TPU v7x, 32 devices: a whole 2x2x4 slice. The times are simulated.
32 devices in a mesh: dp: 4 (over y, core), tensor: 8 (over z, x).
Axes of the slice: x: 2, y: 2, z: 4, core: 2. Of those that a mesh axis runs over, the one named last changes fastest.
Arguments:
- block_input: float32 [4, 2048, 1024], P('dp', 'tensor'), may hold values from -6 to 6
- segment_ids: int32 [4, 2048], P('dp'), may hold values from 0 to 2, as said below
- positions: int32 [4, 2048], P('dp'), may hold values from 0 to 1791, as said below
- attention_gain: bfloat16 [1024], P('dp'), may hold values from 0.099609375 to 1.8984375
- feedforward_gain: bfloat16 [1024], P('dp'), may hold values from 0.099609375 to 1.8984375
- qkv_weight: bfloat16 [1024, 3, 1024], P('dp', None, 'tensor'), may hold values from -2 to 2, as said below
- output_weight: bfloat16 [1024, 1024], P('tensor', 'dp'), may hold values from -0.75 to 0.75
- expand_weight: bfloat16 [1024, 2, 2624], P('dp', None, 'tensor'), may hold values from -0.1875 to 0.1875
- contract_weight: bfloat16 [2624, 1024], P('tensor', 'dp'), may hold values from -0.25 to 0.25
- cotangent: float32 [4, 2048, 1024], P('dp', 'tensor'), may hold values from -6 to 6
Outputs:
- block_output: float32 [4, 2048, 1024], P('dp', 'tensor')
- input_grad: float32 [4, 2048, 1024], P('dp', 'tensor')
- attention_gain_grad: float32 [1024], P('dp')
- feedforward_gain_grad: float32 [1024], P('dp')
- qkv_grad: float32 [1024, 3, 1024], P('dp', None, 'tensor')
- output_grad: float32 [1024, 1024], P('tensor', 'dp')
- expand_grad: float32 [1024, 2, 2624], P('dp', None, 'tensor')
- contract_grad: float32 [2624, 1024], P('tensor', 'dp')
Inputs may be any that keep to these rules, and one draw needn't show every extreme that they name: `segment_ids`: within each sequence the numbers never fall; a token's number tells its document, and a number may be skipped. `positions`: each token's position counts the tokens before it in its own document; no document is longer than 1792 tokens, and some document is that long. `qkv_weight`: the joined query, key and value projection.
All inputs are finite; a program needn't handle non-finite values.
Results may differ from a plain program's by a relative error of at most 0.025.
Values may be sent and summed in bfloat16 or wider, within the bound.
A program may use at most 128 MiB of HBM per device.

v0:
```python
import math

import jax
import jax.numpy as jnp
from jax import lax
from jax.sharding import PartitionSpec as P

HD = 64
WINDOW = 128


EPSILON = 1e-05
MASKED = -1e30
ROOT_HALF = 0.7071067811865476
DENSITY = 0.3989422804014327


def layer_norm(values, gain_vector):
    centre = values - jnp.mean(values, axis=-1, keepdims=True)
    variance = jnp.mean(centre * centre, axis=-1, keepdims=True)
    inverse = lax.rsqrt(variance + EPSILON)
    normed = centre * inverse
    return (normed, inverse, (normed * gain_vector.astype(jnp.float32)).astype(jnp.bfloat16))


def norm_backward(upstream, normed, inverse, gain_vector):
    scaled = upstream * gain_vector.astype(jnp.float32)
    inner_term = (
        scaled
        - jnp.mean(scaled, axis=-1, keepdims=True)
        - normed * jnp.mean(scaled * normed, axis=-1, keepdims=True)
    )
    return (inverse * inner_term, jnp.sum(upstream * normed, axis=0))


def gelu_pair(values):
    normal_cdf = 0.5 * (1.0 + lax.erf(values * ROOT_HALF))
    return (values * normal_cdf, normal_cdf + values * DENSITY * jnp.exp(-0.5 * values * values))


def rope_tables(places, head_size):
    half_size = head_size // 2
    frequency = jnp.exp(
        jnp.arange(half_size, dtype=jnp.float32) * (-2.0 * math.log(10000.0) / head_size)
    )
    angles = places.astype(jnp.float32)[:, None] * frequency[None, :]
    cosine_table = jnp.concatenate([jnp.cos(angles), jnp.cos(angles)], axis=-1)[:, None, :]
    sine_table = jnp.concatenate([jnp.sin(angles), jnp.sin(angles)], axis=-1)[:, None, :]
    return (cosine_table, sine_table)


def rotate(tensor, cosine_table, sine_table):
    half_size = tensor.shape[-1] // 2
    turned = jnp.concatenate([-tensor[..., half_size:], tensor[..., :half_size]], axis=-1)
    return tensor * cosine_table + turned * sine_table


def unrotate(tensor, cosine_table, sine_table):
    half_size = tensor.shape[-1] // 2
    weighted = tensor * sine_table
    turned = jnp.concatenate([weighted[..., half_size:], -weighted[..., :half_size]], axis=-1)
    return tensor * cosine_table + turned


def block_scores(query_block, key_block, segment_query, segment_key, block_rows, scale):
    reach = WINDOW // 2
    scores = (
        jnp.einsum("qhd,khd->hqk", query_block, key_block, preferred_element_type=jnp.float32)
        * scale
    )
    offset = jnp.arange(block_rows)[:, None] + reach - jnp.arange(block_rows + 2 * reach)[None, :]
    valid = (jnp.abs(offset) <= reach) & (segment_query[:, None] == segment_key[None, :])
    return jnp.where(valid[None], scores, MASKED)


def band_pads(keys, values, segments):
    reach = WINDOW // 2
    pad_keys = jnp.pad(keys, ((reach, reach), (0, 0), (0, 0)))
    pad_values = jnp.pad(values, ((reach, reach), (0, 0), (0, 0)))
    pad_segments = jnp.pad(segments, (reach, reach), constant_values=-1)
    return (pad_keys, pad_values, pad_segments)


def band_forward(queries, keys, values, segments):
    length, heads, head_size = queries.shape
    reach = WINDOW // 2
    block = min(length, 512)
    scale = head_size ** (-0.5)
    pad_keys, pad_values, pad_segments = band_pads(keys, values, segments)

    def one_block(index):
        start = index * block
        query_block = lax.dynamic_slice_in_dim(queries, start, block, 0)
        key_block = lax.dynamic_slice_in_dim(pad_keys, start, block + 2 * reach, 0)
        value_block = lax.dynamic_slice_in_dim(pad_values, start, block + 2 * reach, 0)
        segment_query = lax.dynamic_slice_in_dim(segments, start, block, 0)
        segment_key = lax.dynamic_slice_in_dim(pad_segments, start, block + 2 * reach, 0)
        scores = block_scores(query_block, key_block, segment_query, segment_key, block, scale)
        peak = jnp.max(scores, axis=-1, keepdims=True)
        log_total = peak + jnp.log(jnp.sum(jnp.exp(scores - peak), axis=-1, keepdims=True))
        weights = jnp.exp(scores - log_total).astype(jnp.bfloat16)
        context = jnp.einsum(
            "hqk,khd->qhd", weights, value_block, preferred_element_type=jnp.float32
        ).astype(jnp.bfloat16)
        return (context, log_total[..., 0])

    contexts, totals = lax.map(one_block, jnp.arange(length // block, dtype=jnp.int32))
    return (contexts.reshape(length, heads, head_size), totals)


def band_backward(queries, keys, values, segments, grad_context, totals):
    length, heads, head_size = queries.shape
    reach = WINDOW // 2
    block = min(length, 512)
    span = block + 2 * reach
    scale = head_size ** (-0.5)
    pad_keys, pad_values, pad_segments = band_pads(keys, values, segments)

    def one_block(carry, index):
        grad_keys, grad_values = carry
        start = index * block
        query_block = lax.dynamic_slice_in_dim(queries, start, block, 0)
        key_block = lax.dynamic_slice_in_dim(pad_keys, start, span, 0)
        value_block = lax.dynamic_slice_in_dim(pad_values, start, span, 0)
        segment_query = lax.dynamic_slice_in_dim(segments, start, block, 0)
        segment_key = lax.dynamic_slice_in_dim(pad_segments, start, span, 0)
        grad_block = lax.dynamic_slice_in_dim(grad_context, start, block, 0)
        scores = block_scores(query_block, key_block, segment_query, segment_key, block, scale)
        probs = jnp.exp(scores - totals[index][..., None])
        grad_probs = jnp.einsum(
            "qhd,khd->hqk", grad_block, value_block, preferred_element_type=jnp.float32
        )
        delta = jnp.sum(probs * grad_probs, axis=-1, keepdims=True)
        grad_scores = (probs * (grad_probs - delta) * scale).astype(jnp.bfloat16)
        grad_query = jnp.einsum(
            "hqk,khd->qhd", grad_scores, key_block, preferred_element_type=jnp.float32
        )
        key_part = jnp.einsum(
            "hqk,qhd->khd", grad_scores, query_block, preferred_element_type=jnp.float32
        )
        value_part = jnp.einsum(
            "hqk,qhd->khd",
            probs.astype(jnp.bfloat16),
            grad_block,
            preferred_element_type=jnp.float32,
        )
        grad_keys = lax.dynamic_update_slice_in_dim(
            grad_keys, lax.dynamic_slice_in_dim(grad_keys, start, span, 0) + key_part, start, 0
        )
        grad_values = lax.dynamic_update_slice_in_dim(
            grad_values,
            lax.dynamic_slice_in_dim(grad_values, start, span, 0) + value_part,
            start,
            0,
        )
        return ((grad_keys, grad_values), grad_query)

    zeros = jnp.zeros((length + 2 * reach, heads, head_size), jnp.float32)
    (grad_keys, grad_values), grad_queries = lax.scan(
        one_block, (zeros, zeros), jnp.arange(length // block, dtype=jnp.int32)
    )
    return (
        grad_queries.reshape(length, heads, head_size),
        grad_keys[reach : reach + length],
        grad_values[reach : reach + length],
    )


def body(
    block_input,
    segment_ids,
    positions,
    attention_gain,
    feedforward_gain,
    qkv_weight,
    output_weight,
    expand_weight,
    contract_weight,
    cotangent,
):
    batches, local_rows, width = block_input.shape
    head_width = qkv_weight.shape[2]
    heads_here = head_width // HD
    unit_count = expand_weight.shape[2]
    qkv_full, expand_full, output_full, contract_full, first_gain, second_gain = (
        lax.all_gather(qkv_weight, "dp", axis=0, tiled=True),
        lax.all_gather(expand_weight, "dp", axis=0, tiled=True),
        lax.all_gather(output_weight, "dp", axis=1, tiled=True),
        lax.all_gather(contract_weight, "dp", axis=1, tiled=True),
        lax.all_gather(attention_gain, "dp", axis=0, tiled=True),
        lax.all_gather(feedforward_gain, "dp", axis=0, tiled=True),
    )
    qkv_matrix = qkv_full.reshape(width, 3 * head_width)
    expand_matrix = expand_full.reshape(width, 2 * unit_count)
    tokens = block_input[0]
    segments = segment_ids[0]
    cosine_table, sine_table = rope_tables(positions[0], HD)
    normed_one, inverse_one, rounded_one = layer_norm(tokens, first_gain)
    rows_one = lax.all_gather(rounded_one, "tensor", axis=0, tiled=True)
    length_all = rows_one.shape[0]
    projected = jnp.dot(rows_one, qkv_matrix, preferred_element_type=jnp.float32).reshape(
        length_all, 3, heads_here, HD
    )
    queries = rotate(projected[:, 0], cosine_table, sine_table).astype(jnp.bfloat16)
    keys = rotate(projected[:, 1], cosine_table, sine_table).astype(jnp.bfloat16)
    values_in = projected[:, 2].astype(jnp.bfloat16)
    context, totals = band_forward(queries, keys, values_in, segments)
    context_rows = context.reshape(length_all, head_width)
    attended = lax.psum_scatter(
        jnp.dot(context_rows, output_full, preferred_element_type=jnp.float32).astype(jnp.bfloat16),
        "tensor",
        scatter_dimension=0,
        tiled=True,
    ).astype(jnp.float32)
    residual = tokens + attended
    normed_two, inverse_two, rounded_two = layer_norm(residual, second_gain)
    rows_two = lax.all_gather(rounded_two, "tensor", axis=0, tiled=True)
    expanded = jnp.dot(rows_two, expand_matrix, preferred_element_type=jnp.float32).reshape(
        length_all, 2, unit_count
    )
    activated, slope = gelu_pair(expanded[:, 0])
    hidden = (activated * expanded[:, 1]).astype(jnp.bfloat16)
    contracted = lax.psum_scatter(
        jnp.dot(hidden, contract_full, preferred_element_type=jnp.float32).astype(jnp.bfloat16),
        "tensor",
        scatter_dimension=0,
        tiled=True,
    ).astype(jnp.float32)
    results = [residual + contracted]
    upstream = cotangent[0]
    rows_back = lax.all_gather(upstream.astype(jnp.bfloat16), "tensor", axis=0, tiled=True)
    grad_contract = jnp.dot(hidden.T, rows_back, preferred_element_type=jnp.float32)
    grad_hidden = jnp.dot(rows_back, contract_full.T, preferred_element_type=jnp.float32)
    grad_units = (
        jnp.stack([grad_hidden * expanded[:, 1] * slope, grad_hidden * activated], axis=1)
        .astype(jnp.bfloat16)
        .reshape(length_all, 2 * unit_count)
    )
    grad_expand = jnp.dot(rows_two.T, grad_units, preferred_element_type=jnp.float32)
    grad_two = lax.psum_scatter(
        jnp.dot(grad_units, expand_matrix.T, preferred_element_type=jnp.float32).astype(
            jnp.bfloat16
        ),
        "tensor",
        scatter_dimension=0,
        tiled=True,
    ).astype(jnp.float32)
    through_two, gain_part = norm_backward(grad_two, normed_two, inverse_two, second_gain)
    gain_second = gain_part
    grad_mid = upstream + through_two
    rows_mid = lax.all_gather(grad_mid.astype(jnp.bfloat16), "tensor", axis=0, tiled=True)
    grad_output = jnp.dot(context_rows.T, rows_mid, preferred_element_type=jnp.float32)
    grad_context = (
        jnp.dot(rows_mid, output_full.T, preferred_element_type=jnp.float32)
        .astype(jnp.bfloat16)
        .reshape(length_all, heads_here, HD)
    )
    grad_queries, grad_keys, grad_values = band_backward(
        queries, keys, values_in, segments, grad_context, totals
    )
    grad_proj = (
        jnp.stack(
            [
                unrotate(grad_queries, cosine_table, sine_table),
                unrotate(grad_keys, cosine_table, sine_table),
                grad_values,
            ],
            axis=1,
        )
        .astype(jnp.bfloat16)
        .reshape(length_all, 3 * head_width)
    )
    grad_qkv = jnp.dot(rows_one.T, grad_proj, preferred_element_type=jnp.float32)
    grad_one = lax.psum_scatter(
        jnp.dot(grad_proj, qkv_matrix.T, preferred_element_type=jnp.float32).astype(jnp.bfloat16),
        "tensor",
        scatter_dimension=0,
        tiled=True,
    ).astype(jnp.float32)
    through_one, gain_part = norm_backward(grad_one, normed_one, inverse_one, first_gain)
    input_grads = [grad_mid + through_one]
    gains_local = jnp.stack([gain_part, gain_second])
    owned_qkv, owned_expand, owned_output, owned_contract, owned_gains = (
        lax.psum_scatter(
            grad_qkv.reshape(width, 3, head_width).astype(jnp.bfloat16),
            "dp",
            scatter_dimension=0,
            tiled=True,
        ).astype(jnp.float32),
        lax.psum_scatter(
            grad_expand.reshape(width, 2, unit_count).astype(jnp.bfloat16),
            "dp",
            scatter_dimension=0,
            tiled=True,
        ).astype(jnp.float32),
        lax.psum_scatter(
            grad_output.astype(jnp.bfloat16), "dp", scatter_dimension=1, tiled=True
        ).astype(jnp.float32),
        lax.psum_scatter(
            grad_contract.astype(jnp.bfloat16), "dp", scatter_dimension=1, tiled=True
        ).astype(jnp.float32),
        lax.psum_scatter(
            gains_local.astype(jnp.bfloat16), "dp", scatter_dimension=1, tiled=True
        ).astype(jnp.float32),
    )
    gains_total = lax.psum(owned_gains, "tensor")
    return (
        jnp.stack(results),
        jnp.stack(input_grads),
        gains_total[0],
        gains_total[1],
        owned_qkv,
        owned_output,
        owned_expand,
        owned_contract,
    )


def solution(mesh):
    return jax.shard_map(
        body,
        mesh=mesh,
        in_specs=(
            P("dp", "tensor", None),
            P("dp", None),
            P("dp", None),
            P("dp"),
            P("dp"),
            P("dp", None, "tensor"),
            P("tensor", "dp"),
            P("dp", None, "tensor"),
            P("tensor", "dp"),
            P("dp", "tensor", None),
        ),
        out_specs=(
            P("dp", "tensor", None),
            P("dp", "tensor", None),
            P("dp"),
            P("dp"),
            P("dp", None, "tensor"),
            P("tensor", "dp"),
            P("dp", None, "tensor"),
            P("tensor", "dp"),
        ),
        check_vma=False,
    )
```

profile of v0, /device:TPU:0, one launch (start us, length us, event | category | flops | bytes accessed | tf_op | source)
XLA Modules:
  0.0 944.4 jit_solution(6730951717546695902)
XLA Ops:
  11.7 6.0 all-gather
  19.1 6.3 all_gather.33
  26.5 9.2 all_gather.32
  35.6 57.8 %all-gather.8.cloned.1.call-done = bf16[2048,1024]{1,0:T(8,128)(2,1)} async-done(((bf16[256,1024]{1,0:T(8,128)(2,1)}), bf16[2048,1024]{1,0:T(8,128)(2,1)}) %all-gather.8.cloned.1.call-update) | async-done | bytes 4194320 | tf_op jit(solution)/shard_map/all_gather | solution.py:199
  93.5 4.2 fusion.68
  100.9 22.1 %while.26 = (s32[]{:T(128)}, bf16[4,512,2,64]{1,3,2,0:T(8,128)(2,1)S(1)}, f32[4,2,512]{2,1,0:T(2,128)S(1)}, s32[4]{0:T(128)S(1)}, bf16[2176,2,64]{0,2,1:T(8,128)...) while((s32[]{:T(128)}, ...), condition=%wide.region_5.6_spmd, body=%wide.region_2.5_spmd.sunk | while | flops 176684544 | bytes 9815796 | solution.py:107
  124.3 3.2 convolution_convert_fusion.2
  128.2 5.1 all-gather.1
  133.3 81.3 %reduce-scatter.12.cloned.1.call-done = bf16[256,1024]{1,0:T(8,128)(2,1)} async-done(((bf16[2048,1024]{1,0:T(8,128)(2,1)}), bf16[256,1024]{1,0:T(8,128)(2,1)}) %reduce-scatter.12.cloned.1.call-update) | async-done | bytes 524304 | tf_op jit(solution)/shard_map/reduce_scatter | solution.py:209
  219.4 8.1 all_gather.37
  227.5 61.9 %all-gather.10.cloned.1.call-done = bf16[2048,1024]{1,0:T(8,128)(2,1)} async-done(((bf16[256,1024]{1,0:T(8,128)(2,1)}), bf16[2048,1024]{1,0:T(8,128)(2,1)}) %all-gather.10.cloned.1.call-update) | async-done | bytes 4194320 | tf_op jit(solution)/shard_map/all_gather | solution.py:217
  289.4 7.9 fusion.74
  297.4 65.8 %all-gather.14.cloned.1.call-done = bf16[2048,1024]{1,0:T(8,128)(2,1)} async-done(((bf16[256,1024]{1,0:T(8,128)(2,1)}), bf16[2048,1024]{1,0:T(8,128)(2,1)}) %all-gather.14.cloned.1.call-update) | async-done | bytes 4194320 | tf_op jit(solution)/shard_map/all_gather | solution.py:231
  363.2 6.9 fusion.80
  371.6 5.1 bitcast_convert_fusion
  376.8 2.9 multiply_convert_fusion.1
  380.8 4.4 convolution_convert_fusion.1
  385.3 78.5 %reduce-scatter.16.cloned.1.call-done = bf16[256,1024]{1,0:T(8,128)(2,1)} async-done(((bf16[2048,1024]{1,0:T(8,128)(2,1)}), bf16[256,1024]{1,0:T(8,128)(2,1)}) %reduce-scatter.16.cloned.1.call-update) | async-done | bytes 524304 | tf_op jit(solution)/shard_map/reduce_scatter | solution.py:240
  465.3 89.9 %reduce-scatter.14.cloned.1.call-done = bf16[256,1024]{1,0:T(8,128)(2,1)} async-done(((bf16[2048,1024]{1,0:T(8,128)(2,1)}), bf16[256,1024]{1,0:T(8,128)(2,1)}) %reduce-scatter.14.cloned.1.call-update) | async-done | bytes 524304 | tf_op jit(solution)/shard_map/reduce_scatter | solution.py:223
  555.2 3.2 fusion.119
  558.5 5.1 convolution_convert_fusion.4
  563.9 7.0 fusion.83
  570.9 59.8 %all-gather.16.cloned.1.call-done = bf16[2048,1024]{1,0:T(8,128)(2,1)} async-done(((bf16[256,1024]{1,0:T(8,128)(2,1)}), bf16[2048,1024]{1,0:T(8,128)(2,1)}) %all-gather.16.cloned.1.call-update) | async-done | bytes 4194320 | tf_op jit(solution)/shard_map/all_gather | solution.py:251
  630.7 4.5 convolution_convert_fusion.3
  637.4 105.5 %while.27 = (s32[]{:T(128)}, f32[2176,2,64]{0,2,1:T(8,128)}, f32[2176,2,64]{0,2,1:T(8,128)}, f32[4,512,2,64]{1,0,3,2:T(4,128)}, s32[4]{0:T(128)S(1)}, /*index=5*...) while((s32[]{:T(128)}, f32[2176,2,64]{0,2,1:T(8,128)}, ...), condition=%wide.region_15.16_spmd, body=%wide.region_13.15_spmd.sunk | while | flops 430411520 | bytes 33158988 | solution.py:159
  643.2 3.0 fusion.175
  646.2 4.1 fusion.178
  651.5 6.1 dynamic_update_slice.31
  657.6 4.0 fusion.176
  669.6 3.0 fusion.175
  672.6 4.2 fusion.178
  678.0 6.1 dynamic_update_slice.31
  684.2 4.0 fusion.176
  696.1 3.0 fusion.175
  699.1 4.0 fusion.178
  704.3 6.1 dynamic_update_slice.31
  710.5 4.0 fusion.176
  722.4 3.0 fusion.175
  725.4 4.0 fusion.178
  730.6 6.1 dynamic_update_slice.31
  736.7 4.0 fusion.176
  742.9 3.9 convolution_convert_fusion.5
  759.1 3.2 fusion.88
  762.4 5.7 convolution_convert_fusion
  775.9 24.1 %reduce-scatter.20.cloned.1.call-done = bf16[256,3,128]{2,0,1:T(8,128)(2,1)} async-done(((bf16[1024,3,128]{2,0,1:T(8,128)(2,1)}), bf16[256,3,128]{2,0,1:T(8,128)(2,1)}) %reduce-scatter.20.cloned.1.call-update) | async-done | bytes 196624 | tf_op jit(solution)/shard_map/reduce_scatter | solution.py:284
  801.7 90.0 %reduce-scatter.18.cloned.1.call-done = bf16[256,1024]{1,0:T(8,128)(2,1)} async-done(((bf16[2048,1024]{1,0:T(8,128)(2,1)}), bf16[256,1024]{1,0:T(8,128)(2,1)}) %reduce-scatter.18.cloned.1.call-update) | async-done | bytes 524304 | tf_op jit(solution)/shard_map/reduce_scatter | solution.py:274
  896.7 17.3 %reduce-scatter.28.cloned.1.call-done = bf16[256,2]{1,0:T(8,128)(2,1)} async-done(((bf16[1024,2]{1,0:T(8,128)(2,1)}), bf16[256,2]{1,0:T(8,128)(2,1)}) %reduce-scatter.28.cloned.1.call-update) | async-done | bytes 1040
  914.9 21.4 %psum.7 = f32[2,256]{1,0:T(2,128)S(1)} all-reduce(bf16[2,256]{1,0:T(2,128)(2,1)S(1)} %copy.35), channel_id=1, replica_groups=mesh['dp'=4,'tensor'=8] {'tensor'}, use_global_device_ids=true, to_apply=%region_22.23 | all-reduce | flops 512 | bytes 3072 | tf_op jit(solution)/shard_map/psum | solution.py:306
  (218 shorter events, 96.2 us)
Async XLA Ops:
  8.0 9.7 %copy-start = (f32[1,256,1024]{2,1,0:T(8,128)S(1)}, f32[1,256,1024]{2,1,0:T(8,128)}, u32[]{:S(2)}) copy-start(f32[1,256,1024]{2,1,0:T(8,128)} %param.14) | copy-start | bytes 3145732
  8.0 10.8 %copy-start.15 = (bf16[256,3,128]{2,0,1:T(8,128)(2,1)S(1)}, bf16[256,3,128]{2,0,1:T(8,128)(2,1)}, u32[]{:S(2)}) copy-start(bf16[256,3,128]{2,0,1:T(8,128)(2,1)} %param.19) | copy-start | bytes 589828
  8.0 11.0 %copy-start.19 = (s32[1,2048]{1,0:T(1,128)S(1)}, s32[1,2048]{1,0:T(1,128)}, u32[]{:S(2)}) copy-start(s32[1,2048]{1,0:T(1,128)} %param.16) | copy-start | bytes 24580
  8.0 11.0 %copy-start.17 = (s32[1,2048]{1,0:T(1,128)S(1)}, s32[1,2048]{1,0:T(1,128)}, u32[]{:S(2)}) copy-start(s32[1,2048]{1,0:T(1,128)} %param.15) | copy-start | bytes 24580
  8.0 11.1 %copy-start.18 = (bf16[128,256]{1,0:T(8,128)(2,1)S(1)}, bf16[128,256]{1,0:T(8,128)(2,1)}, u32[]{:S(2)}) copy-start(bf16[128,256]{1,0:T(8,128)(2,1)} %param.20) | copy-start | bytes 196612
  8.1 85.4 %all-gather.8.cloned.1.call-start = ((), (), s32[]{:S(2)}) async-start(), calls=%async_computation.9 | async-start | bytes 4718592 | tf_op jit(solution)/shard_map/all_gather | solution.py:199
  18.8 195.8 %reduce-scatter.12.cloned.1.call-start = ((), (), s32[]{:S(2)}) async-start(), calls=%async_computation.10 | async-start | bytes 4718592 | tf_op jit(solution)/shard_map/reduce_scatter | solution.py:209
  26.5 71.7 %copy-start.4 = (f32[2048,64]{0,1:T(8,128)}, f32[2048,64]{0,1:T(8,128)S(1)}, u32[]{:S(2)}) copy-start(f32[2048,64]{0,1:T(8,128)S(1)} %get-tuple-element.205) | copy-start | bytes 1572868
  98.2 2.6 copy-start.14
  123.0 4.6 copy-start.9
  123.5 0.8 copy-start.3
  127.6 0.7 copy-start.22
  127.6 99.9 %all-gather.12.cloned.1.call-start = ((), (), s32[]{:S(2)}) async-start(), calls=%async_computation.12 | async-start | bytes 1679360 | tf_op jit(solution)/shard_map/all_gather | solution.py:187
  128.2 161.2 %all-gather.10.cloned.1.call-start = ((), (), s32[]{:S(2)}) async-start(), calls=%async_computation.11 | async-start | bytes 4718592 | tf_op jit(solution)/shard_map/all_gather | solution.py:217
  215.8 3.5 copy-start.16
  217.1 146.0 %all-gather.14.cloned.1.call-start = ((), (), s32[]{:S(2)}) async-start(), calls=%async_computation.14 | async-start | bytes 4718592 | tf_op jit(solution)/shard_map/all_gather | solution.py:231
  219.3 244.4 %reduce-scatter.16.cloned.1.call-start = ((), (), s32[]{:S(2)}) async-start(), calls=%async_computation.15 | async-start | bytes 4718592 | tf_op jit(solution)/shard_map/reduce_scatter | solution.py:240
  363.2 8.4 copy-start.21
  370.1 1.1 copy-start.23
  370.1 1.5 copy-start.25
  376.7 178.5 %reduce-scatter.14.cloned.1.call-start = ((), (), s32[]{:S(2)}) async-start(), calls=%async_computation.13 | async-start | bytes 4718592 | tf_op jit(solution)/shard_map/reduce_scatter | solution.py:223
  379.7 1.2 copy-start.12
  385.2 170.0 %copy-start.8 = (f32[1,256,1024]{2,1,0:T(8,128)S(1)}, f32[1,256,1024]{2,1,0:T(8,128)}, u32[]{:S(2)}) copy-start(f32[1,256,1024]{2,1,0:T(8,128)} %param.23) | copy-start | bytes 3145732
  385.3 245.5 %all-gather.16.cloned.1.call-start = ((), (), s32[]{:S(2)}) async-start(), calls=%async_computation.16 | async-start | bytes 4718592 | tf_op jit(solution)/shard_map/all_gather | solution.py:251
  558.4 5.5 copy-start.24
  558.4 209.8 %reduce-scatter.26.cloned.1.call-start = ((), (), s32[]{:S(2)}) async-start(), calls=%async_computation.21 | async-start | bytes 839680 | tf_op jit(solution)/shard_map/reduce_scatter | solution.py:299
  563.6 206.4 %reduce-scatter.24.cloned.1.call-start = ((), (), s32[]{:S(2)}) async-start(), calls=%async_computation.20 | async-start | bytes 1679360 | tf_op jit(solution)/shard_map/reduce_scatter | solution.py:290
  570.9 203.5 %reduce-scatter.22.cloned.1.call-start = ((), (), s32[]{:S(2)}) async-start(), calls=%async_computation.19 | async-start | bytes 327680 | tf_op jit(solution)/shard_map/reduce_scatter | solution.py:296
  742.9 3.9 copy-start.7
  746.8 3.7 copy-start.2
  746.8 3.7 copy-start.5
  755.9 1.9 copy-start.10
  755.9 44.1 %reduce-scatter.20.cloned.1.call-start = ((), (), s32[]{:S(2)}) async-start(), calls=%async_computation.18 | async-start | bytes 983040 | tf_op jit(solution)/shard_map/reduce_scatter | solution.py:284
  756.2 2.9 copy-start.20
  757.9 1.1 copy-start.11
  759.1 3.3 copy-start.13
  762.3 129.4 %reduce-scatter.18.cloned.1.call-start = ((), (), s32[]{:S(2)}) async-start(), calls=%async_computation.17 | async-start | bytes 4718592 | tf_op jit(solution)/shard_map/reduce_scatter | solution.py:274
  768.1 123.6 %copy-start.1 = (f32[1,256,1024]{2,1,0:T(8,128)S(1)}, f32[1,256,1024]{2,1,0:T(8,128)}, u32[]{:S(2)}) copy-start(f32[1,256,1024]{2,1,0:T(8,128)} %param.14) | copy-start | bytes 3145732
  768.2 126.1 %copy-start.6 = (f32[256,1024]{1,0:T(8,128)S(1)}, f32[256,1024]{1,0:T(8,128)}, u32[]{:S(2)}) copy-start(f32[256,1024]{1,0:T(8,128)} %get-tuple-element.176) | copy-start | bytes 3145732
  768.2 145.8 %reduce-scatter.28.cloned.1.call-start = ((), (), s32[]{:S(2)}) async-start(), calls=%async_computation.22 | async-start | bytes 327680
Sparse Core Ops, SparseCore 0:
  18.9 74.5 all-gather.7
  127.7 86.8 reduce-scatter.11
  376.8 86.8 reduce-scatter.15
  467.2 87.9 reduce-scatter.13
Sparse Core Ops, SparseCore 1:
  129.6 16.9 all-gather.11
  217.2 72.1 all-gather.9
  292.0 71.1 all-gather.13
  558.5 72.2 all-gather.15
  633.9 21.1 reduce-scatter.25
  657.6 26.5 reduce-scatter.23
  756.0 18.4 reduce-scatter.21
  776.8 23.1 reduce-scatter.19
  803.5 88.2 reduce-scatter.17
  894.3 19.6 reduce-scatter.27
where the time goes:
time: 954 us; the launch traced here: 944 us
  waiting for transfers between devices  630 us (66%)
  matrix products  133 us (14%)
  blocking collectives  56 us (6%)
  local copies, waits for them, and re-layouts  52.7 us (6%)
  other arithmetic  42.4 us (4%)
  between operations  16.3 us (2%)
  loops' own time  13.3 us (1%)
    reduce_scatter x1, waiting for transfers between devices, body(): lax.psum_scatter(jnp.dot(grad_proj, qkv_matrix.T, preferred_element_type=...  90 us
    reduce_scatter x1, waiting for transfers between devices, body(): lax.psum_scatter(jnp.dot(hidden, contract_full, preferred_element_type=jn...  89.9 us
    reduce_scatter x1, waiting for transfers between devices, body(): lax.psum_scatter(jnp.dot(context_rows, output_full, preferred_element_typ...  81.3 us
    reduce_scatter x1, waiting for transfers between devices, body(): lax.psum_scatter(jnp.dot(grad_units, expand_matrix.T, preferred_element_t...  78.5 us
    all_gather x1, waiting for transfers between devices, body(): lax.all_gather(upstream.astype(jnp.bfloat16), 'tensor', axis=0, tiled=True)  65.8 us
    all_gather x1, waiting for transfers between devices, body(): rows_two = lax.all_gather(rounded_two, 'tensor', axis=0, tiled=True)  61.9 us
    all_gather x1, waiting for transfers between devices, body(): lax.all_gather(grad_mid.astype(jnp.bfloat16), 'tensor', axis=0, tiled=True)  59.8 us
    all_gather x1, waiting for transfers between devices, body(): rows_one = lax.all_gather(rounded_one, 'tensor', axis=0, tiled=True)  57.8 us
  transfers between devices with their start and end apart: 14, of which 11 were waited for; matrix products, arithmetic and copies ran while one was open for 18% of the time, Pallas kernels for 0%

commit v1 on v0

v1 whole, which is shorter than its diff:
```python
import functools
import math

import jax
import jax.numpy as jnp
from jax import lax
from jax.experimental import pallas as pl
from jax.experimental.pallas import tpu as pltpu
from jax.sharding import PartitionSpec as P

HD = 64
WINDOW = 128
REACH = WINDOW // 2
EPSILON = 1e-05
MASKED = -1e30
ROOT_HALF = 0.7071067811865476
DENSITY = 0.3989422804014327
BOTH = ("dp", "tensor")
GAIN_ROWS = 16
CHUNKS = 2
NN = (((1,), (0,)), ((), ()))
NT = (((1,), (1,)), ((), ()))
TN = (((0,), (0,)), ((), ()))


def mm(left, right, dims):
    return lax.dot_general(left, right, dims, preferred_element_type=jnp.float32)


def norm_rows(values):
    centre = values - jnp.mean(values, axis=-1, keepdims=True)
    variance = jnp.mean(centre * centre, axis=-1, keepdims=True)
    inverse = lax.rsqrt(variance + EPSILON)
    return centre * inverse, inverse


def norm_back(upstream, normed, inverse, gain):
    scaled = upstream * gain
    inner = (
        scaled
        - jnp.mean(scaled, axis=-1, keepdims=True)
        - normed * jnp.mean(scaled * normed, axis=-1, keepdims=True)
    )
    return inverse * inner


def wide(ref, part):
    return jnp.concatenate([ref[d, 0, part] for d in range(ref.shape[0])], axis=1)


def spread(ref, part, value):
    rows = ref.shape[-1]
    for d in range(ref.shape[0]):
        ref[d, 0, part] = value[:, d * rows : (d + 1) * rows].astype(ref.dtype)


def turn(tensor, first_sign):
    half = HD // 2
    pieces = []
    for head in range(tensor.shape[1] // HD):
        low = tensor[:, head * HD : head * HD + half]
        high = tensor[:, head * HD + half : (head + 1) * HD]
        pieces += [-high, low] if first_sign < 0 else [high, -low]
    return jnp.concatenate(pieces, axis=1)


def blocks_of(tokens):
    size = min(tokens, 128)
    return [(start, size, size + 2 * REACH) for start in range(0, tokens, size)]


def band_mask(segq, segk, start, size, span):
    rows = lax.broadcasted_iota(jnp.int32, (size, span), 0)
    cols = lax.broadcasted_iota(jnp.int32, (size, span), 1)
    near = jnp.abs(rows + REACH - cols) <= REACH
    return near & (segq[start : start + size, :] == segk[:, start : start + span])


def attend_kernel(x_ref, gain_ref, w_ref, cos_ref, sin_ref, segq_ref, segk_ref,
                  y_ref, qkv_ref, ctx_ref, lse_ref, a_ref):
    step = pl.program_id(0)
    tokens = y_ref.shape[0]
    scale = HD ** (-0.5)

    @pl.when(step == 0)
    def _():
        normed, _ = norm_rows(x_ref[...])
        a_ref[...] = (normed * gain_ref[...].astype(jnp.float32)).astype(jnp.bfloat16)
        y_ref[...] = x_ref[REACH : REACH + tokens, :]

    a = a_ref[...]
    cos, sin = cos_ref[...], sin_ref[...]
    q = mm(a, wide(w_ref, 0), NT)
    k = mm(a, wide(w_ref, 1), NT)
    v = mm(a, wide(w_ref, 2), NT).astype(jnp.bfloat16)
    q = (q * cos + turn(q, -1) * sin).astype(jnp.bfloat16)
    k = (k * cos + turn(k, -1) * sin).astype(jnp.bfloat16)
    qkv_ref[0, 0], qkv_ref[0, 1], qkv_ref[0, 2] = q, k, v
    heads = q.shape[1] // HD
    segq, segk = segq_ref[...], segk_ref[...]
    contexts, totals = [], []
    for start, size, span in blocks_of(tokens):
        valid = band_mask(segq, segk, start, size, span)
        row_ctx, row_lse = [], []
        for head in range(heads):
            lanes = slice(head * HD, (head + 1) * HD)
            qb = q[REACH + start : REACH + start + size, lanes]
            kb = k[start : start + span, lanes]
            vb = v[start : start + span, lanes]
            s = jnp.where(valid, mm(qb, kb, NT) * scale, MASKED)
            peak = jnp.max(s, axis=-1, keepdims=True)
            total = peak + jnp.log(jnp.sum(jnp.exp(s - peak), axis=-1, keepdims=True))
            weights = jnp.exp(s - total).astype(jnp.bfloat16)
            row_ctx.append(mm(weights, vb, NN))
            row_lse.append(total)
        contexts.append(jnp.concatenate(row_ctx, axis=1))
        totals.append(jnp.concatenate(row_lse, axis=1))
    context = jnp.concatenate(contexts, axis=0).astype(jnp.bfloat16)
    ctx_ref[0] = context
    lse_ref[0] = jnp.concatenate(totals, axis=0)
    y_ref[...] += mm(context, wide(w_ref, 3), NN)


def attend_back_kernel(x_ref, gain_ref, w_ref, cos_ref, sin_ref, segq_ref, segk_ref,
                       qkv_ref, ctx_ref, lse_ref, dy_ref,
                       dw_ref, da_ref, gg_ref, a_ref, n_ref, d_ref):
    step = pl.program_id(0)
    tokens = dy_ref.shape[0]
    scale = HD ** (-0.5)

    @pl.when(step == 0)
    def _():
        normed, _ = norm_rows(x_ref[...])
        n_ref[...] = normed
        a_ref[...] = (normed * gain_ref[...].astype(jnp.float32)).astype(jnp.bfloat16)
        d_ref[...] = dy_ref[...].astype(jnp.bfloat16)
        da_ref[...] = jnp.zeros_like(da_ref)

    dyb = d_ref[...]
    dc = mm(dyb, wide(w_ref, 3), NT).astype(jnp.bfloat16)
    spread(dw_ref, 3, mm(ctx_ref[0], dyb, TN))
    q, k, v = qkv_ref[0, 0], qkv_ref[0, 1], qkv_ref[0, 2]
    heads = q.shape[1] // HD
    segq, segk = segq_ref[...], segk_ref[...]
    lse = lse_ref[0]
    extent = tokens + 2 * REACH
    width = q.shape[1]
    dq_rows = []
    dk = jnp.zeros((extent, width), jnp.float32)
    dv = jnp.zeros((extent, width), jnp.float32)
    for start, size, span in blocks_of(tokens):
        valid = band_mask(segq, segk, start, size, span)
        dq_parts, dk_parts, dv_parts = [], [], []
        for head in range(heads):
            lanes = slice(head * HD, (head + 1) * HD)
            qb = q[REACH + start : REACH + start + size, lanes]
            kb = k[start : start + span, lanes]
            vb = v[start : start + span, lanes]
            db = dc[start : start + size, lanes]
            s = jnp.where(valid, mm(qb, kb, NT) * scale, MASKED)
            probs = jnp.exp(s - lse[start : start + size, head : head + 1])
            dp = mm(db, vb, NT)
            delta = jnp.sum(probs * dp, axis=-1, keepdims=True)
            ds = (probs * (dp - delta) * scale).astype(jnp.bfloat16)
            dq_parts.append(mm(ds, kb, NN))
            dk_parts.append(mm(ds, qb, TN))
            dv_parts.append(mm(probs.astype(jnp.bfloat16), db, TN))
        dq_rows.append(jnp.concatenate(dq_parts, axis=1))
        pads = ((start, extent - start - span), (0, 0))
        for parts, which in ((dk_parts, 0), (dv_parts, 1)):
            block = jnp.concatenate(parts, axis=1)
            rows = []
            if pads[0][0]:
                rows.append(jnp.zeros((pads[0][0], width), jnp.float32))
            rows.append(block)
            if pads[0][1]:
                rows.append(jnp.zeros((pads[0][1], width), jnp.float32))
            block = jnp.concatenate(rows, axis=0) if len(rows) > 1 else block
            if which == 0:
                dk = dk + block
            else:
                dv = dv + block
    cos, sin = cos_ref[...], sin_ref[...]
    dq = jnp.concatenate(dq_rows, axis=0)
    inner = slice(REACH, REACH + tokens)
    dq = (dq * cos[inner] + turn(dq * sin[inner], 1)).astype(jnp.bfloat16)
    dk = (dk * cos + turn(dk * sin, 1)).astype(jnp.bfloat16)
    dv = dv.astype(jnp.bfloat16)
    a = a_ref[...]
    spread(dw_ref, 0, mm(dq, a[inner], TN))
    spread(dw_ref, 1, mm(dk, a, TN))
    spread(dw_ref, 2, mm(dv, a, TN))
    da_ref[...] += mm(dk, wide(w_ref, 1), NN) + mm(dv, wide(w_ref, 2), NN)
    da_ref[inner, :] += mm(dq, wide(w_ref, 0), NN)

    @pl.when(step == pl.num_programs(0) - 1)
    def _():
        gg_ref[...] = jnp.sum(da_ref[...] * n_ref[...], axis=0, keepdims=True)


def feed_kernel(y_ref, gain_ref, up_ref, w_ref, out0_ref, da0_ref,
                dw_ref, out_ref, da_ref, a_ref, u_ref):
    step = pl.program_id(0)

    @pl.when(step == 0)
    def _():
        normed, _ = norm_rows(y_ref[...])
        a_ref[...] = (normed * gain_ref[...].astype(jnp.float32)).astype(jnp.bfloat16)
        u_ref[...] = up_ref[...].astype(jnp.bfloat16)
        out_ref[...] = out0_ref[...]
        da_ref[...] = da0_ref[...]

    a, up = a_ref[...], u_ref[...]
    w0, w1, c = wide(w_ref, 0), wide(w_ref, 1), wide(w_ref, 2)
    u0 = mm(w0, a, NT)
    u1 = mm(w1, a, NT)
    cdf = 0.5 * (1.0 + lax.erf(u0 * ROOT_HALF))
    activated = u0 * cdf
    slope = cdf + u0 * DENSITY * jnp.exp(-0.5 * u0 * u0)
    hidden = (activated * u1).astype(jnp.bfloat16)
    out_ref[...] += mm(hidden, c, TN)
    spread(dw_ref, 2, mm(hidden, up, NN))
    dg = mm(c, up, NT)
    du0 = (dg * u1 * slope).astype(jnp.bfloat16)
    du1 = (dg * activated).astype(jnp.bfloat16)
    spread(dw_ref, 0, mm(du0, a, NN))
    spread(dw_ref, 1, mm(du1, a, NN))
    da_ref[...] += mm(du0, w0, TN) + mm(du1, w1, TN)


def full_spec(shape):
    return pl.BlockSpec(shape, lambda t: (0,) * len(shape))


def weight_spec(shape):
    return pl.BlockSpec(
        (shape[0], 1) + shape[2:], lambda t: (0, t) + (0,) * (len(shape) - 2)
    )


def lead_spec(shape):
    return pl.BlockSpec((1,) + shape[1:], lambda t: (t,) + (0,) * (len(shape) - 1))


def params():
    return pltpu.CompilerParams(
        dimension_semantics=("arbitrary",), vmem_limit_bytes=56 * 1024 * 1024
    )


def shaped(shape, dtype):
    return jax.ShapeDtypeStruct(shape, dtype)


def cost(flops, moved):
    return pl.CostEstimate(flops=int(flops), bytes_accessed=int(moved), transcendentals=0)


def body(
    dps,
    tensors,
    block_input,
    segment_ids,
    positions,
    attention_gain,
    feedforward_gain,
    qkv_weight,
    output_weight,
    expand_weight,
    contract_weight,
    cotangent,
):
    tokens, width = block_input.shape[1:]
    rows = qkv_weight.shape[0]
    hw = qkv_weight.shape[2]
    units = contract_weight.shape[0]
    heads = hw // HD
    extent = tokens + 2 * REACH
    f32, bf16 = jnp.float32, jnp.bfloat16

    x = block_input[0]
    upstream = cotangent[0]
    place = lax.axis_index("tensor")
    ahead = [(i, i + 1) for i in range(tensors - 1)]
    behind = [(i + 1, i) for i in range(tensors - 1)]
    before = lax.ppermute(x[tokens - REACH :], "tensor", ahead)
    after = lax.ppermute(x[:REACH], "tensor", behind)
    x_ext = jnp.concatenate([before, x, after], axis=0)

    gains = jnp.stack([attention_gain, feedforward_gain])
    first = jnp.concatenate(
        [
            jnp.transpose(qkv_weight, (1, 2, 0)).reshape(3 * hw, rows),
            output_weight,
            jnp.pad(gains, ((0, GAIN_ROWS - 2), (0, 0))),
        ],
        axis=0,
    )
    got_first = lax.all_gather(first, BOTH, axis=0, tiled=False).reshape(
        dps, tensors, 4 * hw + GAIN_ROWS, rows
    )
    stacked = jnp.concatenate(
        [jnp.transpose(expand_weight, (1, 2, 0)), contract_weight[None]], axis=0
    )
    cut = -(-units // (8 * CHUNKS)) * 8
    edges = [min(i * cut, units) for i in range(CHUNKS + 1)]
    got_feed = [
        lax.all_gather(stacked[:, lo:hi], BOTH, axis=0, tiled=False).reshape(
            dps, tensors, 3, hi - lo, rows
        )
        for lo, hi in zip(edges[:-1], edges[1:])
    ]
    gain_rows = got_first[:, 0, 4 * hw : 4 * hw + 2]
    gain_one = gain_rows[:, 0].reshape(1, width)
    gain_two = gain_rows[:, 1].reshape(1, width)
    w_attn = got_first[:, :, : 4 * hw].reshape(dps, tensors, 4, hw, rows)

    seg_all = jnp.pad(segment_ids[0], (REACH, REACH), constant_values=-1)
    pos_all = jnp.pad(positions[0], (REACH, REACH))
    seg_k = lax.dynamic_slice_in_dim(seg_all, place * tokens, extent, 0)
    pos = lax.dynamic_slice_in_dim(pos_all, place * tokens, extent, 0)
    seg_q = seg_k[REACH : REACH + tokens]
    half = HD // 2
    frequency = jnp.exp(jnp.arange(half, dtype=f32) * (-2.0 * math.log(10000.0) / HD))
    angles = pos.astype(f32)[:, None] * frequency[None, :]
    cos = jnp.tile(jnp.cos(angles), (1, 2 * heads))
    sin = jnp.tile(jnp.sin(angles), (1, 2 * heads))
    seg_q, seg_k = seg_q[:, None], seg_k[None, :]

    w_shape = w_attn.shape
    side = [
        full_spec((extent, width)),
        full_spec((1, width)),
        weight_spec(w_shape),
        full_spec((extent, hw)),
        full_spec((extent, hw)),
        full_spec((tokens, 1)),
        full_spec((1, extent)),
    ]
    qkv_shape = (tensors, 3, extent, hw)
    ctx_shape = (tensors, tokens, hw)
    lse_shape = (tensors, tokens, heads)
    attn_flops = 2 * tensors * extent * 4 * hw * width
    attn_bytes = 2 * 4 * width * width
    y, qkv, ctx, lse = pl.pallas_call(
        attend_kernel,
        grid=(tensors,),
        in_specs=side,
        out_specs=[
            full_spec((tokens, width)),
            lead_spec(qkv_shape),
            lead_spec(ctx_shape),
            lead_spec(lse_shape),
        ],
        out_shape=[
            shaped((tokens, width), f32),
            shaped(qkv_shape, bf16),
            shaped(ctx_shape, bf16),
            shaped(lse_shape, f32),
        ],
        scratch_shapes=[pltpu.VMEM((extent, width), bf16)],
        compiler_params=params(),
        cost_estimate=cost(attn_flops, attn_bytes),
        name="attend",
    )(x_ext, gain_one, w_attn, cos, sin, seg_q, seg_k)

    out, da_two = y, jnp.zeros((tokens, width), f32)
    owned_feed = []
    for got in got_feed:
        size = got.shape[3]
        dw, out, da_two = pl.pallas_call(
            feed_kernel,
            grid=(tensors,),
            in_specs=[
                full_spec((tokens, width)),
                full_spec((1, width)),
                full_spec((tokens, width)),
                weight_spec(got.shape),
                full_spec((tokens, width)),
                full_spec((tokens, width)),
            ],
            out_specs=[
                weight_spec(got.shape),
                full_spec((tokens, width)),
                full_spec((tokens, width)),
            ],
            out_shape=[
                shaped(got.shape, bf16),
                shaped((tokens, width), f32),
                shaped((tokens, width), f32),
            ],
            scratch_shapes=[
                pltpu.VMEM((tokens, width), bf16),
                pltpu.VMEM((tokens, width), bf16),
            ],
            compiler_params=params(),
            cost_estimate=cost(18 * tensors * tokens * size * width, 12 * tensors * size * width),
            name="feed",
        )(y, gain_two, upstream, got, out, da_two)
        owned_feed.append(
            lax.psum_scatter(
                dw.reshape((dps * tensors,) + got.shape[2:]),
                BOTH,
                scatter_dimension=0,
                tiled=True,
            )[0]
        )

    normed_two, inverse_two = norm_rows(y)
    gain_grad_two = jnp.sum(da_two * normed_two, axis=0)
    grad_mid = upstream + norm_back(da_two, normed_two, inverse_two, gain_two.astype(f32))

    dw_shape = (dps, tensors, 4 * hw + GAIN_ROWS, rows)
    dw_view = (dps, tensors, 4, hw, rows)
    dw_attn, da_one, gain_grad_one = pl.pallas_call(
        attend_back_kernel,
        grid=(tensors,),
        in_specs=side
        + [
            lead_spec(qkv_shape),
            lead_spec(ctx_shape),
            lead_spec(lse_shape),
            full_spec((tokens, width)),
        ],
        out_specs=[
            weight_spec(dw_view),
            full_spec((extent, width)),
            full_spec((1, width)),
        ],
        out_shape=[
            shaped(dw_view, bf16),
            shaped((extent, width), f32),
            shaped((1, width), f32),
        ],
        scratch_shapes=[
            pltpu.VMEM((extent, width), bf16),
            pltpu.VMEM((extent, width), f32),
            pltpu.VMEM((tokens, width), bf16),
        ],
        compiler_params=params(),
        cost_estimate=cost(2 * attn_flops, 2 * attn_bytes),
        name="attend_back",
    )(x_ext, gain_one, w_attn, cos, sin, seg_q, seg_k, qkv, ctx, lse, grad_mid)

    gain_grads = jnp.stack([gain_grad_one[0], gain_grad_two]).reshape(2, dps, rows)
    gain_block = jnp.broadcast_to(
        jnp.pad(jnp.transpose(gain_grads, (1, 0, 2)), ((0, 0), (0, GAIN_ROWS - 2), (0, 0)))[
            :, None
        ],
        (dps, tensors, GAIN_ROWS, rows),
    ).astype(bf16)
    last = jnp.concatenate(
        [dw_attn.reshape(dps, tensors, 4 * hw, rows), gain_block], axis=2
    ).reshape((dps * tensors,) + dw_shape[2:])
    owned = lax.psum_scatter(last, BOTH, scatter_dimension=0, tiled=True)[0]

    to_before = lax.ppermute(da_one[:REACH].astype(bf16), "tensor", behind).astype(f32)
    to_after = lax.ppermute(da_one[tokens + REACH :].astype(bf16), "tensor", ahead).astype(f32)
    da_total = da_one[REACH : REACH + tokens]
    da_total = da_total + jnp.concatenate(
        [to_after, jnp.zeros((tokens - 2 * REACH, width), f32), to_before], axis=0
    )
    normed_one, inverse_one = norm_rows(x)
    input_grad = grad_mid + norm_back(da_total, normed_one, inverse_one, gain_one.astype(f32))

    feed = jnp.concatenate(owned_feed, axis=1)
    return (
        out[None],
        input_grad[None],
        owned[4 * hw].astype(f32),
        owned[4 * hw + 1].astype(f32),
        jnp.transpose(owned[: 3 * hw].reshape(3, hw, rows), (2, 0, 1)).astype(f32),
        owned[3 * hw : 4 * hw].astype(f32),
        jnp.transpose(feed[:2], (2, 0, 1)).astype(f32),
        feed[2].astype(f32),
    )


def solution(mesh):
    return jax.shard_map(
        functools.partial(body, mesh.shape["dp"], mesh.shape["tensor"]),
        mesh=mesh,
        in_specs=(
            P("dp", "tensor", None),
            P("dp", None),
            P("dp", None),
            P("dp"),
            P("dp"),
            P("dp", None, "tensor"),
            P("tensor", "dp"),
            P("dp", None, "tensor"),
            P("tensor", "dp"),
            P("dp", "tensor", None),
        ),
        out_specs=(
            P("dp", "tensor", None),
            P("dp", "tensor", None),
            P("dp"),
            P("dp"),
            P("dp", None, "tensor"),
            P("tensor", "dp"),
            P("dp", None, "tensor"),
            P("tensor", "dp"),
        ),
        check_vma=False,
    )
```

time: 954 us -> 683 us (0.72)
  matrix products: 133 us -> 0 us
  waiting for transfers between devices: 630 us -> 512 us
  Pallas kernels: 0 us -> 94.5 us
  blocking collectives: 56 us -> 0 us
  local copies, waits for them, and re-layouts: 52.7 us -> 20.2 us
  loops' own time: 13.3 us -> 0 us
  other arithmetic: 42.4 us -> 29.5 us
  starting transfers between devices: 1.06 us -> 11.3 us
    dot_general x40 -> x0, matrix products: 133 us -> none  [the longest x4 16.4 us: one_block(): jnp.einsum('hqk,khd->qhd', grad_scores, key_block, preferred_element_type...]
    pallas_call x0 -> x4, Pallas kernels: none -> 94.5 us  [the longest x2 40.4 us: body(): pl.pallas_call(feed_kernel, grid=(tensors,), in_specs=[full_spec((tokens,...]
    all_gather x5 -> x3, waiting for transfers between devices: 245 us -> 162 us  [the longest x2 101 us: body(): lax.all_gather(stacked[:, lo:hi], BOTH, axis=0, tiled=False)]
    all_gather x5 -> x0, blocking collectives: 34.6 us -> none  [the longest x1 9.15 us: body(): lax.all_gather(qkv_weight, 'dp', axis=0, tiled=True)]
    reduce_scatter x8 -> x3, waiting for transfers between devices: 366 us -> 334 us  [the longest x2 200 us: body(): lax.psum_scatter(dw.reshape((dps * tensors,) + got.shape[2:]), BOTH, scat...]
    dynamic_update_slice x8 -> x0, local copies, waits for them, and re-layouts: 29.4 us -> none  [band_backward(): lax.scan(one_block, (zeros, zeros), jnp.arange(length // block, dtype=jnp...]
    psum x1 -> x0, blocking collectives: 21.4 us -> none  [body(): gains_total = lax.psum(owned_gains, 'tensor')]
    unnamed x15 -> x6, waiting for transfers between devices: 18 us -> 0.62 us
  transfers between devices with their start and end apart: 14 -> 10, of which waited for: 11 -> 9; matrix products, arithmetic and copies ran while one was open for 18% -> 6% of each run, Pallas kernels for 0% -> 11%
where the time goes in v1:
time: 683 us; the launch traced here: 682 us
  waiting for transfers between devices  512 us (75%)
  Pallas kernels  94.5 us (14%)
  other arithmetic  29.5 us (4%)
  local copies, waits for them, and re-layouts  20.2 us (3%)
  between operations  14.3 us (2%)
  starting transfers between devices  11.3 us (2%)
    reduce_scatter x2, waiting for transfers between devices, body(): lax.psum_scatter(dw.reshape((dps * tensors,) + got.shape[2:]), BOTH, scat...  200 us
    reduce_scatter x1, waiting for transfers between devices, body(): owned = lax.psum_scatter(last, BOTH, scatter_dimension=0, tiled=True)[0]  134 us
    all_gather x2, waiting for transfers between devices, body(): lax.all_gather(stacked[:, lo:hi], BOTH, axis=0, tiled=False)  101 us
    all_gather x1, waiting for transfers between devices, body(): lax.all_gather(first, BOTH, axis=0, tiled=False)  60.3 us
    pallas_call x2, Pallas kernels, body(): pl.pallas_call(feed_kernel, grid=(tensors,), in_specs=[full_spec((tokens,...  40.4 us
    pallas_call x1, Pallas kernels, body(): pl.pallas_call(attend_back_kernel, grid=(tensors,), in_specs=side + [lead...  30.2 us
    pallas_call x1, Pallas kernels, body(): pl.pallas_call(attend_kernel, grid=(tensors,), in_specs=side, out_specs=[...  23.9 us
  transfers between devices with their start and end apart: 10, of which 9 were waited for; matrix products, arithmetic and copies ran while one was open for 6% of the time, Pallas kernels for 11%

profile of v1, /device:TPU:0, one launch (start us, length us, event | category | flops | bytes accessed | tf_op | source)
XLA Modules:
  0.0 682.1 jit_solution(5771487356829727422)
XLA Ops:
  7.2 1.1 copy.29
  8.3 0.7 stack.17
  8.9 0.7 stack.18
  9.6 1.6 pad_maximum_fusion.2
  11.2 1.7 pad_maximum_fusion.3
  13.0 1.7 pad_maximum_fusion.4
  14.7 1.1 slice_bitcast_fusion.1
  15.8 4.9 collective-permute-start
  20.7 1.3 collective-permute-start.1
  22.0 0.8 fusion.8
  22.8 0.8 pad_dynamic-slice_fusion
  23.7 0.5 broadcast_in_dim.17.segk_ref
  24.4 0.8 copy.30.cos_ref
  25.3 0.8 copy.31.sin_ref
  26.1 0.8 copy.32.segq_ref
  26.9 6.9 %collective-permute-done = f32[64,1024]{1,0:T(8,128)S(1)} collective-permute-done((f32[64,1024]{1,0:T(8,128)S(1)}, f32[64,1024]{1,0:T(8,128)S(1)}, u32[]{:S(2)}, u32[]{:S(2)}) %collective-permute-start) | collective-permute-done | bytes 262176 | tf_op jit(solution)/shard_map/ppermute | solution.py:286
  33.8 2.6 pad_maximum_fusion.1.x_ref
  36.4 60.3 %all-gather.7.cloned.1.call-done = bf16[16896,256]{1,0:T(8,128)(2,1)} async-done(((bf16[528,256]{1,0:T(8,128)(2,1)}), bf16[16896,256]{1,0:T(8,128)(2,1)}) %all-gather.7.cloned.1.call-update) | async-done | bytes 8650768 | tf_op jit(solution)/shard_map/all_gather | solution.py:299
  96.7 7.5 %slice.88 = bf16[4,8,512,256]{3,2,1,0:T(8,128)(2,1)} slice(bf16[4,8,528,256]{3,2,1,0:T(8,128)(2,1)} %bitcast.63), slice={[0:4], [0:8], [0:512], [0:256]} | slice | bytes 16777216 | tf_op jit(solution)/shard_map/slice | solution.py:316
  104.2 0.7 slice_bitcast_fusion.3
  104.9 0.6 slice_convert_fusion.3
  105.5 23.9 %attend.1 = (f32[256,1024]{1,0:T(8,128)}, bf16[8,3,384,128]{3,2,1,0:T(8,128)(2,1)}, bf16[8,256,128]{2,1,0:T(8,128)(2,1)}, f32[8,256,2]{2,1,0:T(8,128)}) custom-call(f32[384,1024]{1,0:T(8,128)} %pad_maximum_fusion.1.x_ref, bf16[1,1024]{1,0:T(2,128)(2,1)} %bitcast.89, bf16[4,8,4,128,256]{4,3,2,1,0:T(8,128)(2,1)} %bitcast.59, f32[384,128]{1,0:T(8,128)} %copy.30.cos_ref, ...), custom_call_target="tpu_custom_call" | custom-call | flops 3221225472 | bytes 8388608 | tf_op jit(solution)/shard_map/attend/pallas_call | solution.py:345
  129.4 46.2 %all-gather.11.cloned.1.call-done = bf16[96,168,256]{2,1,0:T(8,128)(2,1)} async-done(((bf16[3,168,256]{2,1,0:T(8,128)(2,1)}), bf16[96,168,256]{2,1,0:T(8,128)(2,1)}) %all-gather.11.cloned.1.call-update) | async-done | bytes 8257552 | tf_op jit(solution)/shard_map/all_gather | solution.py:308
  175.6 1.1 broadcast_in_dim.19.da0_ref
  176.7 20.5 %feed.2 = (bf16[4,8,3,168,256]{4,3,2,1,0:T(8,128)(2,1)}, f32[256,1024]{1,0:T(8,128)}, f32[256,1024]{1,0:T(8,128)}) custom-call(f32[256,1024]{1,0:T(8,128)} %get-tuple-element.21.y_ref.out0_ref, bf16[1,1024]{1,0:T(2,128)(2,1)} %bitcast.91, f32[256,1024]{1,0:T(8,128)} %bitcast.69, bf16[4,8,3,168,256]{4,3,2,1,0:T(8,128)(2,1)} %bitcast.95, ...), custom_call_target="tpu_custom_call" | custom-call | flops 6341787648 | bytes 16515072 | tf_op jit(solution)/shard_map/feed/pallas_call | solution.py:371
  197.1 55.2 %all-gather.9.cloned.1.call-done = bf16[96,160,256]{2,1,0:T(8,128)(2,1)} async-done(((bf16[3,160,256]{2,1,0:T(8,128)(2,1)}), bf16[96,160,256]{2,1,0:T(8,128)(2,1)}) %all-gather.9.cloned.1.call-update) | async-done | bytes 7864336 | tf_op jit(solution)/shard_map/all_gather | solution.py:308
  252.4 20.0 %feed.3 = (bf16[4,8,3,160,256]{4,3,2,1,0:T(8,128)(2,1)}, f32[256,1024]{1,0:T(8,128)}, f32[256,1024]{1,0:T(8,128)}) custom-call(f32[256,1024]{1,0:T(8,128)} %get-tuple-element.21.y_ref.out0_ref, bf16[1,1024]{1,0:T(2,128)(2,1)} %bitcast.92, f32[256,1024]{1,0:T(8,128)} %bitcast.70, bf16[4,8,3,160,256]{4,3,2,1,0:T(8,128)(2,1)} %bitcast.96, ...), custom_call_target="tpu_custom_call" | custom-call | flops 6039797760 | bytes 15728640 | tf_op jit(solution)/shard_map/feed/pallas_call | solution.py:371
  272.5 0.5 reduce-scatter.6.cloned.1.call-update
  274.0 0.5 multiply_reduce_fusion
  274.5 1.3 multiply_add_fusion.dy_ref
  275.8 30.2 %attend_back.1 = (bf16[4,8,4,128,256]{4,3,2,1,0:T(8,128)(2,1)}, f32[384,1024]{1,0:T(8,128)}, f32[1,1024]{1,0:T(1,128)}) custom-call(f32[384,1024]{1,0:T(8,128)} %pad_maximum_fusion.1.x_ref, bf16[1,1024]{1,0:T(2,128)(2,1)} %bitcast.90, bf16[4,8,4,128,256]{4,3,2,1,0:T(8,128)(2,1)} %bitcast.60, f32[384,128]{1,0:T(8,128)} %copy.30.cos_ref, ...), custom_call_target="tpu_custom_call" | custom-call | flops 6442450944 | bytes 16777216 | tf_op jit(solution)/shard_map/attend_back/pallas_call | solution.py:415
  306.0 0.7 convert_reduce_fusion
  306.8 7.4 %pad_maximum_fusion = bf16[32,528,256]{2,1,0:T(8,128)(2,1)} fusion(bf16[32,16,256]{2,1,0:T(8,128)(2,1)S(1)} %bitcast.68, bf16[32,512,256]{2,1,0:T(8,128)(2,1)} %bitcast.61), kind=kLoop, calls=%fused_computation | loop fusion | flops 17301504 | bytes 17301504 | tf_op jit(solution)/shard_map/concatenate | solution.py:452
  314.3 1.2 copy-done
  316.1 3.4 collective-permute-start.2
  319.5 1.3 collective-permute-start.3
  320.8 1.9 collective-permute-done.2
  322.8 6.8 %collective-permute-done.3 = bf16[64,1024]{1,0:T(8,128)(2,1)S(1)} collective-permute-done((bf16[64,1024]{1,0:T(8,128)(2,1)S(1)}, bf16[64,1024]{1,0:T(8,128)(2,1)S(1)}, u32[]{:S(2)}, u32[]{:S(2)}) %collective-permute-start.3) | collective-permute-done | bytes 131104 | tf_op jit(solution)/shard_map/ppermute | solution.py:457
  330.1 2.6 add_bitcast_fusion
  332.8 64.3 %reduce-scatter.8.cloned.1.call-done = bf16[1,3,160,256]{3,2,1,0:T(8,128)(2,1)} async-done(((bf16[32,3,160,256]{3,2,1,0:T(8,128)(2,1)}), bf16[1,3,160,256]{3,2,1,0:T(8,128)(2,1)}) %reduce-scatter.8.cloned.1.call-update) | async-done | bytes 245776 | tf_op jit(solution)/shard_map/reduce_scatter | solution.py:401
  397.1 136.0 %reduce-scatter.6.cloned.1.call-done = bf16[1,3,168,256]{3,2,1,0:T(8,128)(2,1)} async-done(((bf16[32,3,168,256]{3,2,1,0:T(8,128)(2,1)}), bf16[1,3,168,256]{3,2,1,0:T(8,128)(2,1)}) %reduce-scatter.6.cloned.1.call-update) | async-done | bytes 258064 | tf_op jit(solution)/shard_map/reduce_scatter | solution.py:401
  533.1 1.7 fusion.3
  534.8 1.9 convert_bitcast_fusion
  536.7 134.0 %reduce-scatter.4.cloned.1.call-done = bf16[1,528,256]{2,1,0:T(8,128)(2,1)} async-done(((bf16[32,528,256]{2,1,0:T(8,128)(2,1)}), bf16[1,528,256]{2,1,0:T(8,128)(2,1)}) %reduce-scatter.4.cloned.1.call-update) | async-done | bytes 270352 | tf_op jit(solution)/shard_map/reduce_scatter | solution.py:455
  670.6 0.9 slice.94
  671.6 0.9 copy.37
  672.5 1.5 fusion.4
  674.0 1.3 slice_convert_fusion
  (51 shorter events, 2.9 us)
Async XLA Ops:
  7.2 89.5 %all-gather.7.cloned.1.call-start = ((), (), s32[]{:S(2)}) async-start(), calls=%async_computation.6 | async-start | bytes 8921088 | tf_op jit(solution)/shard_map/all_gather | solution.py:299
  11.2 164.4 %all-gather.11.cloned.1.call-start = ((), (), s32[]{:S(2)}) async-start(), calls=%async_computation.8 | async-start | bytes 8515584 | tf_op jit(solution)/shard_map/all_gather | solution.py:308
  12.9 239.4 %all-gather.9.cloned.1.call-start = ((), (), s32[]{:S(2)}) async-start(), calls=%async_computation.7 | async-start | bytes 8110080 | tf_op jit(solution)/shard_map/all_gather | solution.py:308
  14.7 382.4 %reduce-scatter.8.cloned.1.call-start = ((), (), s32[]{:S(2)}) async-start(), calls=%async_computation.5 | async-start | bytes 8110080 | tf_op jit(solution)/shard_map/reduce_scatter | solution.py:401
  15.8 18.0 %collective-permute-start = (f32[64,1024]{1,0:T(8,128)S(1)}, f32[64,1024]{1,0:T(8,128)S(1)}, u32[]{:S(2)}, u32[]{:S(2)}) collective-permute-start(f32[64,1024]{1,0:T(8,128)S(1)} %get-tuple-element.39), channel_id=1, source_target_pairs={{0,1},{1,2},{2,3},{3,4},{4,5},{5,6},{6,7},{8,9},{9,10},{10,11},{11... | collective-permute-start | bytes 786440 | tf_op jit(solution)/shard_map/ppermute | solution.py:286
  20.7 13.1 %collective-permute-start.1 = (f32[64,1024]{1,0:T(8,128)S(1)}, f32[64,1024]{1,0:T(8,128)S(1)}, u32[]{:S(2)}, u32[]{:S(2)}) collective-permute-start(f32[64,1024]{1,0:T(8,128)S(1)} %get-tuple-element.40), channel_id=1, source_target_pairs={{1,0},{2,1},{3,2},{4,3},{5,4},{6,5},{7,6},{9,8},{10,9},{11,10},{12... | collective-permute-start | bytes 786440 | tf_op jit(solution)/shard_map/ppermute | solution.py:287
  272.4 1.2 copy-start.1
  272.4 1.6 copy-start.3
  272.4 2.1 copy-start.4
  272.4 260.7 %reduce-scatter.6.cloned.1.call-start = ((), (), s32[]{:S(2)}) async-start(), calls=%async_computation.4 | async-start | bytes 8515584 | tf_op jit(solution)/shard_map/reduce_scatter | solution.py:401
  273.0 397.6 %reduce-scatter.4.cloned.1.call-start = ((), (), s32[]{:S(2)}) async-start(), calls=%async_computation.3 | async-start | bytes 8921088 | tf_op jit(solution)/shard_map/reduce_scatter | solution.py:455
  314.2 1.2 copy-start
  314.2 1.7 copy-start.2
  316.1 6.7 collective-permute-start.2
  319.5 10.1 %collective-permute-start.3 = (bf16[64,1024]{1,0:T(8,128)(2,1)S(1)}, bf16[64,1024]{1,0:T(8,128)(2,1)S(1)}, u32[]{:S(2)}, u32[]{:S(2)}) collective-permute-start(bf16[64,1024]{1,0:T(8,128)(2,1)S(1)} %get-tuple-element.42), channel_id=1, source_target_pairs={{1,0},{2,1},{3,2},{4,3},{5,4},{6,5},{7,6},{9,8},{10,9},{11,10},{12... | collective-permute-start | bytes 393224 | tf_op jit(solution)/shard_map/ppermute | solution.py:457
Sparse Core Ops, SparseCore 0:
  11.5 85.1 all-gather.6
  100.3 75.2 all-gather.10
  178.6 73.7 all-gather.8
  272.5 124.5 reduce-scatter.7
  402.8 130.1 reduce-scatter.5
  538.9 131.7 reduce-scatter.3

commit v2 on v1

--- a/solution.py
+++ b/solution.py
@@ -44,14 +44,226 @@
     return inverse * inner
 
 
-def wide(ref, part):
-    return jnp.concatenate([ref[d, 0, part] for d in range(ref.shape[0])], axis=1)
-
-
-def spread(ref, part, value):
+def plans(dps, tensors):
+    dp_bits = [("dp", j) for j in range(dps.bit_length() - 1)]
+    t_bits = [("tensor", j) for j in range(tensors.bit_length() - 1)]
+    core, ys = dp_bits[:1], dp_bits[1:]
+    xs, z_near, z_far = t_bits[:1], t_bits[1:2], t_bits[2:]
+    return (
+        core + ys + xs + z_near + z_far,
+        core + xs + z_near + ys + z_far,
+        core + z_near + ys + xs + z_far,
+        core + ys + xs + z_near + z_far,
+    )
+
+
+def at_block(order, d):
+    return tuple((d >> j) & 1 if axis == "dp" else 0 for axis, j in order)
+
+
+def wide(order, dps, ref, part):
+    return jnp.concatenate([ref[at_block(order, d) + (part,)] for d in range(dps)], axis=1)
+
+
+def spread(order, dps, ref, part, value):
     rows = ref.shape[-1]
-    for d in range(ref.shape[0]):
-        ref[d, 0, part] = value[:, d * rows : (d + 1) * rows].astype(ref.dtype)
+    for d in range(dps):
+        ref[at_block(order, d) + (part,)] = value[:, d * rows : (d + 1) * rows].astype(ref.dtype)
+
+
+def bit_of(axis, j):
+    return (lax.axis_index(axis) // 2**j) % 2
+
+
+def partner(axis, j):
+    moved = {name: lax.axis_index(name) for name in BOTH}
+    moved[axis] = moved[axis] + 2**j * (1 - 2 * bit_of(axis, j))
+    return tuple(moved[name] for name in BOTH)
+
+
+def greet(order):
+    barrier = pltpu.get_barrier_semaphore()
+    for axis, j in order:
+        pl.semaphore_signal(
+            barrier, inc=1, device_id=partner(axis, j), device_id_type=pl.DeviceIdType.MESH
+        )
+    pl.semaphore_wait(barrier, len(order))
+
+
+def gather_kernel(orders, *refs):
+    count = len(orders)
+    ins, outs = refs[:count], refs[count : 2 * count]
+    load_sem, send_sem, recv_sem = refs[2 * count :]
+    bits = len(orders[0])
+    greet(orders[0])
+    spots = []
+    for i, order in enumerate(orders):
+        spot = 0
+        for s, (axis, j) in enumerate(order):
+            spot = spot + bit_of(axis, j) * 2 ** (bits - 1 - s)
+        spots.append(spot)
+    loads = [
+        pltpu.make_async_copy(ins[i], outs[i].at[pl.ds(spots[i], 1)], load_sem.at[i])
+        for i in range(count)
+    ]
+    for load in loads:
+        load.start()
+    for s in range(bits - 1, -1, -1):
+        size = 2 ** (bits - 1 - s)
+        copies = []
+        for i, order in enumerate(orders):
+            base = (spots[i] // size) * size
+            span = outs[i].at[pl.ds(base, size)]
+            copy = pltpu.make_async_remote_copy(
+                src_ref=ins[i] if size == 1 else span,
+                dst_ref=span,
+                send_sem=send_sem.at[i, s],
+                recv_sem=recv_sem.at[i, s],
+                device_id=partner(*order[s]),
+                device_id_type=pl.DeviceIdType.MESH,
+            )
+            copy.start()
+            copies.append(copy)
+        if s == bits - 1:
+            for load in loads:
+                load.wait()
+        for copy in copies:
+            copy.wait()
+
+
+def gather_all(orders, dps, tensors, shards):
+    bits = len(orders[0])
+    group = dps * tensors
+    count = len(shards)
+    return pl.pallas_call(
+        functools.partial(gather_kernel, orders),
+        in_specs=[pl.BlockSpec(memory_space=pltpu.VMEM)] * count,
+        out_specs=[pl.BlockSpec(memory_space=pl.ANY)] * count,
+        out_shape=[jax.ShapeDtypeStruct((group,) + x.shape, x.dtype) for x in shards],
+        scratch_shapes=[
+            pltpu.SemaphoreType.DMA((count,)),
+            pltpu.SemaphoreType.DMA((count, bits)),
+            pltpu.SemaphoreType.DMA((count, bits)),
+        ],
+        compiler_params=pltpu.CompilerParams(collective_id=0, has_side_effects=True),
+        name="gather_all",
+    )(*[x[None] for x in shards])
+
+
+def scatter_kernel(orders, *refs):
+    count = len(orders)
+    bits = len(orders[0])
+    ins, outs = refs[:count], refs[count : 2 * count]
+    lands, owns = refs[2 * count : 3 * count], refs[3 * count : 4 * count]
+    load_sem, send_sem, recv_sem = refs[4 * count :]
+    greet(orders[0])
+    sizes = [2 ** (bits - 1 - s) for s in range(bits)]
+    offsets = [sum(sizes[:s]) for s in range(bits)]
+
+    def send(i, s, base):
+        axis, j = orders[i][s]
+        other = base + (1 - bit_of(axis, j)) * sizes[s]
+        source = ins[i] if s == 0 else lands[i]
+        copy = pltpu.make_async_remote_copy(
+            src_ref=source.at[pl.ds(other, sizes[s])],
+            dst_ref=lands[i].at[pl.ds(offsets[s], sizes[s])],
+            send_sem=send_sem.at[i, s],
+            recv_sem=recv_sem.at[i, s],
+            device_id=partner(axis, j),
+            device_id_type=pl.DeviceIdType.MESH,
+        )
+        copy.start()
+        return copy
+
+    def add(i, s, base, first, size):
+        def one(k, carry):
+            mine = lands[i][base + first + k].astype(jnp.float32)
+            theirs = lands[i][offsets[s] + first + k].astype(jnp.float32)
+            lands[i][base + first + k] = (mine + theirs).astype(lands[i].dtype)
+            return carry
+
+        lax.fori_loop(0, size, one, 0)
+
+    copies = [send(i, 0, 0) for i in range(count)]
+    piece = owns[0].shape[1]
+    pieces = sizes[0] // piece
+
+    def start_of(i, c):
+        return ((1 - bit_of(*orders[i][1])) * sizes[1] + c * piece) % sizes[0]
+
+    def load(i, c):
+        kept = bit_of(*orders[i][0]) * sizes[0] + start_of(i, c)
+        copy = pltpu.make_async_copy(
+            ins[i].at[pl.ds(kept, piece)], owns[i].at[c % 2], load_sem.at[i, c % 2]
+        )
+        copy.start()
+        return copy
+
+    loads = [[load(i, c) for c in range(2)] for i in range(count)]
+    for copy in copies:
+        copy.wait()
+    later = []
+    for c in range(pieces):
+        for i in range(count):
+            loads[i][c].wait()
+            at = start_of(i, c)
+
+            def one(k, carry, i=i, c=c, at=at):
+                mine = owns[i][c % 2, k].astype(jnp.float32)
+                theirs = lands[i][at + k].astype(jnp.float32)
+                lands[i][at + k] = (mine + theirs).astype(lands[i].dtype)
+                return carry
+
+            lax.fori_loop(0, piece, one, 0)
+            if c + 2 < pieces:
+                loads[i].append(load(i, c + 2))
+            if c == pieces // 2 - 1:
+                later.append(send(i, 1, 0))
+    bases = [bit_of(*orders[i][1]) * sizes[1] for i in range(count)]
+    copies = later
+    for s in range(1, bits):
+        later = []
+        for i in range(count):
+            copies[i].wait()
+            if s == bits - 1:
+                mine = lands[i][bases[i]].astype(jnp.float32)
+                theirs = lands[i][offsets[s]].astype(jnp.float32)
+                outs[i][...] = mine + theirs
+                continue
+            bit = bit_of(*orders[i][s + 1])
+            half = sizes[s + 1]
+            add(i, s, bases[i], (1 - bit) * half, half)
+            later.append(send(i, s + 1, bases[i]))
+        for i in range(count):
+            if s < bits - 1:
+                bit = bit_of(*orders[i][s + 1])
+                half = sizes[s + 1]
+                add(i, s, bases[i], bit * half, half)
+                bases[i] = bases[i] + bit * half
+        copies = later
+
+
+def scatter_all(orders, dps, tensors, parts):
+    bits = len(orders[0])
+    group = dps * tensors
+    count = len(parts)
+    return pl.pallas_call(
+        functools.partial(scatter_kernel, orders),
+        in_specs=[pl.BlockSpec(memory_space=pl.ANY)] * count,
+        out_specs=[pl.BlockSpec(memory_space=pltpu.VMEM)] * count,
+        out_shape=[jax.ShapeDtypeStruct(x.shape[1:], jnp.float32) for x in parts],
+        scratch_shapes=[pltpu.VMEM((group - 1,) + x.shape[1:], x.dtype) for x in parts]
+        + [pltpu.VMEM((2, max(group // 16, 1)) + x.shape[1:], x.dtype) for x in parts]
+        + [
+            pltpu.SemaphoreType.DMA((count, 2)),
+            pltpu.SemaphoreType.DMA((count, bits)),
+            pltpu.SemaphoreType.DMA((count, bits)),
+        ],
+        compiler_params=pltpu.CompilerParams(
+            collective_id=1, has_side_effects=True, vmem_limit_bytes=60 * 1024 * 1024
+        ),
+        name="scatter_all",
+    )(*parts)
 
 
 def turn(tensor, first_sign):
@@ -76,7 +288,7 @@
     return near & (segq[start : start + size, :] == segk[:, start : start + span])
 
 
-def attend_kernel(x_ref, gain_ref, w_ref, cos_ref, sin_ref, segq_ref, segk_ref,
+def attend_kernel(order, dps, x_ref, gain_ref, w_ref, cos_ref, sin_ref, segq_ref, segk_ref,
                   y_ref, qkv_ref, ctx_ref, lse_ref, a_ref):
     step = pl.program_id(0)
     tokens = y_ref.shape[0]
@@ -90,9 +302,9 @@
 
     a = a_ref[...]
     cos, sin = cos_ref[...], sin_ref[...]
-    q = mm(a, wide(w_ref, 0), NT)
-    k = mm(a, wide(w_ref, 1), NT)
-    v = mm(a, wide(w_ref, 2), NT).astype(jnp.bfloat16)
+    q = mm(a, wide(order, dps, w_ref, 0), NT)
+    k = mm(a, wide(order, dps, w_ref, 1), NT)
+    v = mm(a, wide(order, dps, w_ref, 2), NT).astype(jnp.bfloat16)
     q = (q * cos + turn(q, -1) * sin).astype(jnp.bfloat16)
     k = (k * cos + turn(k, -1) * sin).astype(jnp.bfloat16)
     qkv_ref[0, 0], qkv_ref[0, 1], qkv_ref[0, 2] = q, k, v
@@ -118,10 +330,10 @@
     context = jnp.concatenate(contexts, axis=0).astype(jnp.bfloat16)
     ctx_ref[0] = context
     lse_ref[0] = jnp.concatenate(totals, axis=0)
-    y_ref[...] += mm(context, wide(w_ref, 3), NN)
-
-
-def attend_back_kernel(x_ref, gain_ref, w_ref, cos_ref, sin_ref, segq_ref, segk_ref,
+    y_ref[...] += mm(context, wide(order, dps, w_ref, 3), NN)
+
+
+def attend_back_kernel(order, dps, x_ref, gain_ref, w_ref, cos_ref, sin_ref, segq_ref, segk_ref,
                        qkv_ref, ctx_ref, lse_ref, dy_ref,
                        dw_ref, da_ref, gg_ref, a_ref, n_ref, d_ref):
     step = pl.program_id(0)
@@ -137,8 +349,8 @@
         da_ref[...] = jnp.zeros_like(da_ref)
 
     dyb = d_ref[...]
-    dc = mm(dyb, wide(w_ref, 3), NT).astype(jnp.bfloat16)
-    spread(dw_ref, 3, mm(ctx_ref[0], dyb, TN))
+    dc = mm(dyb, wide(order, dps, w_ref, 3), NT).astype(jnp.bfloat16)
+    spread(order, dps, dw_ref, 3, mm(ctx_ref[0], dyb, TN))
     q, k, v = qkv_ref[0, 0], qkv_ref[0, 1], qkv_ref[0, 2]
     heads = q.shape[1] // HD
     segq, segk = segq_ref[...], segk_ref[...]
@@ -187,18 +399,18 @@
     dk = (dk * cos + turn(dk * sin, 1)).astype(jnp.bfloat16)
     dv = dv.astype(jnp.bfloat16)
     a = a_ref[...]
-    spread(dw_ref, 0, mm(dq, a[inner], TN))
-    spread(dw_ref, 1, mm(dk, a, TN))
-    spread(dw_ref, 2, mm(dv, a, TN))
-    da_ref[...] += mm(dk, wide(w_ref, 1), NN) + mm(dv, wide(w_ref, 2), NN)
-    da_ref[inner, :] += mm(dq, wide(w_ref, 0), NN)
+    spread(order, dps, dw_ref, 0, mm(dq, a[inner], TN))
+    spread(order, dps, dw_ref, 1, mm(dk, a, TN))
+    spread(order, dps, dw_ref, 2, mm(dv, a, TN))
+    da_ref[...] += mm(dk, wide(order, dps, w_ref, 1), NN) + mm(dv, wide(order, dps, w_ref, 2), NN)
+    da_ref[inner, :] += mm(dq, wide(order, dps, w_ref, 0), NN)
 
     @pl.when(step == pl.num_programs(0) - 1)
     def _():
         gg_ref[...] = jnp.sum(da_ref[...] * n_ref[...], axis=0, keepdims=True)
 
 
-def feed_kernel(y_ref, gain_ref, up_ref, w_ref, out0_ref, da0_ref,
+def feed_kernel(order, dps, y_ref, gain_ref, up_ref, w_ref, out0_ref, da0_ref,
                 dw_ref, out_ref, da_ref, a_ref, u_ref):
     step = pl.program_id(0)
 
@@ -211,7 +423,7 @@
         da_ref[...] = da0_ref[...]
 
     a, up = a_ref[...], u_ref[...]
-    w0, w1, c = wide(w_ref, 0), wide(w_ref, 1), wide(w_ref, 2)
+    w0, w1, c = wide(order, dps, w_ref, 0), wide(order, dps, w_ref, 1), wide(order, dps, w_ref, 2)
     u0 = mm(w0, a, NT)
     u1 = mm(w1, a, NT)
     cdf = 0.5 * (1.0 + lax.erf(u0 * ROOT_HALF))
@@ -219,12 +431,12 @@
     slope = cdf + u0 * DENSITY * jnp.exp(-0.5 * u0 * u0)
     hidden = (activated * u1).astype(jnp.bfloat16)
     out_ref[...] += mm(hidden, c, TN)
-    spread(dw_ref, 2, mm(hidden, up, NN))
+    spread(order, dps, dw_ref, 2, mm(hidden, up, NN))
     dg = mm(c, up, NT)
     du0 = (dg * u1 * slope).astype(jnp.bfloat16)
     du1 = (dg * activated).astype(jnp.bfloat16)
-    spread(dw_ref, 0, mm(du0, a, NN))
-    spread(dw_ref, 1, mm(du1, a, NN))
+    spread(order, dps, dw_ref, 0, mm(du0, a, NN))
+    spread(order, dps, dw_ref, 1, mm(du1, a, NN))
     da_ref[...] += mm(du0, w0, TN) + mm(du1, w1, TN)
 
 
@@ -232,10 +444,13 @@
     return pl.BlockSpec(shape, lambda t: (0,) * len(shape))
 
 
-def weight_spec(shape):
-    return pl.BlockSpec(
-        (shape[0], 1) + shape[2:], lambda t: (0, t) + (0,) * (len(shape) - 2)
-    )
+def weight_spec(order, block):
+    lead = tuple(2 if axis == "dp" else 1 for axis, _ in order)
+
+    def place(t):
+        return tuple(0 if axis == "dp" else (t // 2**j) % 2 for axis, j in order) + (0,) * len(block)
+
+    return pl.BlockSpec(lead + block, place)
 
 
 def lead_spec(shape):
@@ -287,33 +502,27 @@
     after = lax.ppermute(x[:REACH], "tensor", behind)
     x_ext = jnp.concatenate([before, x, after], axis=0)
 
-    gains = jnp.stack([attention_gain, feedforward_gain])
+    orders = plans(dps, tensors)
+    group = dps * tensors
+    bits = len(orders[0])
+    split = (2,) * bits
+    gains = jnp.pad(jnp.stack([attention_gain, feedforward_gain]), ((0, GAIN_ROWS - 2), (0, 0)))
     first = jnp.concatenate(
-        [
-            jnp.transpose(qkv_weight, (1, 2, 0)).reshape(3 * hw, rows),
-            output_weight,
-            jnp.pad(gains, ((0, GAIN_ROWS - 2), (0, 0))),
-        ],
-        axis=0,
-    )
-    got_first = lax.all_gather(first, BOTH, axis=0, tiled=False).reshape(
-        dps, tensors, 4 * hw + GAIN_ROWS, rows
+        [jnp.transpose(qkv_weight, (1, 2, 0)), output_weight[None]], axis=0
     )
     stacked = jnp.concatenate(
         [jnp.transpose(expand_weight, (1, 2, 0)), contract_weight[None]], axis=0
     )
     cut = -(-units // (8 * CHUNKS)) * 8
     edges = [min(i * cut, units) for i in range(CHUNKS + 1)]
-    got_feed = [
-        lax.all_gather(stacked[:, lo:hi], BOTH, axis=0, tiled=False).reshape(
-            dps, tensors, 3, hi - lo, rows
-        )
-        for lo, hi in zip(edges[:-1], edges[1:])
-    ]
-    gain_rows = got_first[:, 0, 4 * hw : 4 * hw + 2]
-    gain_one = gain_rows[:, 0].reshape(1, width)
-    gain_two = gain_rows[:, 1].reshape(1, width)
-    w_attn = got_first[:, :, : 4 * hw].reshape(dps, tensors, 4, hw, rows)
+    shards = [first] + [stacked[:, lo:hi] for lo, hi in zip(edges[:-1], edges[1:])] + [gains]
+    got_first, *got_feed, got_gains = gather_all(orders, dps, tensors, shards)
+    w_attn = got_first.reshape(split + first.shape)
+    at_zero = jnp.stack(
+        [got_gains.reshape(split + gains.shape)[at_block(orders[3], d)] for d in range(dps)]
+    )
+    gain_one = at_zero[:, 0].reshape(1, width)
+    gain_two = at_zero[:, 1].reshape(1, width)
 
     seg_all = jnp.pad(segment_ids[0], (REACH, REACH), constant_values=-1)
     pos_all = jnp.pad(positions[0], (REACH, REACH))
@@ -327,11 +536,11 @@
     sin = jnp.tile(jnp.sin(angles), (1, 2 * heads))
     seg_q, seg_k = seg_q[:, None], seg_k[None, :]
 
-    w_shape = w_attn.shape
+    w_block = first.shape
     side = [
         full_spec((extent, width)),
         full_spec((1, width)),
-        weight_spec(w_shape),
+        weight_spec(orders[0], w_block),
         full_spec((extent, hw)),
         full_spec((extent, hw)),
         full_spec((tokens, 1)),
@@ -343,7 +552,7 @@
     attn_flops = 2 * tensors * extent * 4 * hw * width
     attn_bytes = 2 * 4 * width * width
     y, qkv, ctx, lse = pl.pallas_call(
-        attend_kernel,
+        functools.partial(attend_kernel, orders[0], dps),
         grid=(tensors,),
         in_specs=side,
         out_specs=[
@@ -365,22 +574,24 @@
     )(x_ext, gain_one, w_attn, cos, sin, seg_q, seg_k)
 
     out, da_two = y, jnp.zeros((tokens, width), f32)
-    owned_feed = []
-    for got in got_feed:
-        size = got.shape[3]
+    feed_grads = []
+    for order, got in zip(orders[1:], got_feed):
+        block = got.shape[1:]
+        size = block[1]
+        got = got.reshape(split + block)
         dw, out, da_two = pl.pallas_call(
-            feed_kernel,
+            functools.partial(feed_kernel, order, dps),
             grid=(tensors,),
             in_specs=[
                 full_spec((tokens, width)),
                 full_spec((1, width)),
                 full_spec((tokens, width)),
-                weight_spec(got.shape),
+                weight_spec(order, block),
                 full_spec((tokens, width)),
                 full_spec((tokens, width)),
             ],
             out_specs=[
-                weight_spec(got.shape),
+                weight_spec(order, block),
                 full_spec((tokens, width)),
                 full_spec((tokens, width)),
             ],
@@ -397,23 +608,14 @@
             cost_estimate=cost(18 * tensors * tokens * size * width, 12 * tensors * size * width),
             name="feed",
         )(y, gain_two, upstream, got, out, da_two)
-        owned_feed.append(
-            lax.psum_scatter(
-                dw.reshape((dps * tensors,) + got.shape[2:]),
-                BOTH,
-                scatter_dimension=0,
-                tiled=True,
-            )[0]
-        )
+        feed_grads.append(dw.reshape((group,) + block))
 
     normed_two, inverse_two = norm_rows(y)
     gain_grad_two = jnp.sum(da_two * normed_two, axis=0)
     grad_mid = upstream + norm_back(da_two, normed_two, inverse_two, gain_two.astype(f32))
 
-    dw_shape = (dps, tensors, 4 * hw + GAIN_ROWS, rows)
-    dw_view = (dps, tensors, 4, hw, rows)
     dw_attn, da_one, gain_grad_one = pl.pallas_call(
-        attend_back_kernel,
+        functools.partial(attend_back_kernel, orders[0], dps),
         grid=(tensors,),
         in_specs=side
         + [
@@ -423,12 +625,12 @@
             full_spec((tokens, width)),
         ],
         out_specs=[
-            weight_spec(dw_view),
+            weight_spec(orders[0], w_block),
             full_spec((extent, width)),
             full_spec((1, width)),
         ],
         out_shape=[
-            shaped(dw_view, bf16),
+            shaped(split + w_block, bf16),
             shaped((extent, width), f32),
             shaped((1, width), f32),
         ],
@@ -443,16 +645,19 @@
     )(x_ext, gain_one, w_attn, cos, sin, seg_q, seg_k, qkv, ctx, lse, grad_mid)
 
     gain_grads = jnp.stack([gain_grad_one[0], gain_grad_two]).reshape(2, dps, rows)
+    gain_block = jnp.pad(jnp.transpose(gain_grads, (1, 0, 2)), ((0, 0), (0, 6), (0, 0)))
+    gain_block = gain_block.reshape(
+        tuple(2 for _ in range(dps.bit_length() - 1)) + (1,) * (tensors.bit_length() - 1) + (8, rows)
+    )
+    names = [("dp", j) for j in range(dps.bit_length() - 2, -1, -1)]
+    names += [("tensor", j) for j in range(tensors.bit_length() - 2, -1, -1)]
+    spots = [names.index(bit) for bit in orders[3]]
     gain_block = jnp.broadcast_to(
-        jnp.pad(jnp.transpose(gain_grads, (1, 0, 2)), ((0, 0), (0, GAIN_ROWS - 2), (0, 0)))[
-            :, None
-        ],
-        (dps, tensors, GAIN_ROWS, rows),
-    ).astype(bf16)
-    last = jnp.concatenate(
-        [dw_attn.reshape(dps, tensors, 4 * hw, rows), gain_block], axis=2
-    ).reshape((dps * tensors,) + dw_shape[2:])
-    owned = lax.psum_scatter(last, BOTH, scatter_dimension=0, tiled=True)[0]
+        jnp.transpose(gain_block, spots + [bits, bits + 1]), split + (8, rows)
+    ).reshape(group, 8, rows)
+    owned, *owned_feed, owned_gains = scatter_all(
+        orders, dps, tensors, [dw_attn.reshape((group,) + w_block)] + feed_grads + [gain_block]
+    )
 
     to_before = lax.ppermute(da_one[:REACH].astype(bf16), "tensor", behind).astype(f32)
     to_after = lax.ppermute(da_one[tokens + REACH :].astype(bf16), "tensor", ahead).astype(f32)
@@ -467,12 +672,12 @@
     return (
         out[None],
         input_grad[None],
-        owned[4 * hw].astype(f32),
-        owned[4 * hw + 1].astype(f32),
-        jnp.transpose(owned[: 3 * hw].reshape(3, hw, rows), (2, 0, 1)).astype(f32),
-        owned[3 * hw : 4 * hw].astype(f32),
-        jnp.transpose(feed[:2], (2, 0, 1)).astype(f32),
-        feed[2].astype(f32),
+        owned_gains[0],
+        owned_gains[1],
+        jnp.transpose(owned[:3], (2, 0, 1)),
+        owned[3],
+        jnp.transpose(feed[:2], (2, 0, 1)),
+        feed[2],
     )
 
 

time: 683 us -> 429 us (0.63)
  waiting for transfers between devices: 512 us -> 1.27 us
  Pallas kernels: 94.5 us -> 381 us
  other arithmetic: 29.5 us -> 15.9 us
  between operations: 14.3 us -> 1.01 us
    reduce_scatter x3 -> x0, waiting for transfers between devices: 334 us -> none  [the longest x2 200 us: body(): lax.psum_scatter(dw.reshape((dps * tensors,) + got.shape[2:]), BOTH, scat...]
    pallas_call x4 -> x6, Pallas kernels: 94.5 us -> 381 us  [the longest x1 145 us: gather_all(): pl.pallas_call(functools.partial(gather_kernel, orders), in_specs=[pl.Blo...]
    all_gather x3 -> x0, waiting for transfers between devices: 162 us -> none  [the longest x2 101 us: body(): lax.all_gather(stacked[:, lo:hi], BOTH, axis=0, tiled=False)]
    concatenate x3 -> x0, other arithmetic: 10.6 us -> none  [the longest x1 7.41 us: body(): jnp.concatenate([dw_attn.reshape(dps, tensors, 4 * hw, rows), gain_block]...]
    slice x2 -> x1, local copies, waits for them, and re-layouts: 8.44 us -> 1.34 us  [body(): owned_gains[1]]
    ppermute x1, waiting for transfers between devices: 6.92 us -> 0.01 us  [body(): before = lax.ppermute(x[tokens - REACH:], 'tensor', ahead)]
  transfers between devices with their start and end apart: 10 -> 4, of which waited for: 9 -> 1; matrix products, arithmetic and copies ran while one was open for 6% -> 3% of each run, Pallas kernels for 11% -> 34%
where the time goes in v2:
time: 429 us; the launch traced here: 427 us
  Pallas kernels  381 us (89%)
  other arithmetic  15.9 us (4%)
  local copies, waits for them, and re-layouts  15.5 us (4%)
  starting transfers between devices  12.7 us (3%)
    pallas_call x1, Pallas kernels, gather_all(): pl.pallas_call(functools.partial(gather_kernel, orders), in_specs=[pl.Blo...  145 us
    pallas_call x1, Pallas kernels, scatter_all(): pl.pallas_call(functools.partial(scatter_kernel, orders), in_specs=[pl.Bl...  141 us
    pallas_call x2, Pallas kernels, body(): pl.pallas_call(functools.partial(feed_kernel, order, dps), grid=(tensors,...  41.3 us
    pallas_call x1, Pallas kernels, body(): pl.pallas_call(functools.partial(attend_back_kernel, orders[0], dps), gri...  30.4 us
    pallas_call x1, Pallas kernels, body(): pl.pallas_call(functools.partial(attend_kernel, orders[0], dps), grid=(te...  24 us
  transfers between devices with their start and end apart: 4, of which 1 were waited for; matrix products, arithmetic and copies ran while one was open for 3% of the time, Pallas kernels for 34%

profile of v2, /device:TPU:0, one launch (start us, length us, event | category | flops | bytes accessed | tf_op | source)
XLA Modules:
  0.0 427.5 jit_solution(2008025339998162826)
XLA Ops:
  0.7 1.1 slice_bitcast_fusion.4
  1.8 1.3 collective-permute-start.1
  3.1 5.5 %collective-permute-start = (f32[64,1024]{1,0:T(8,128)S(1)}, f32[64,1024]{1,0:T(8,128)S(1)}, u32[]{:S(2)}, u32[]{:S(2)}) collective-permute-start(f32[64,1024]{1,0:T(8,128)S(1)} %get-tuple-element.75), channel_id=1, source_target_pairs={{0,1},{1,2},{2,3},{3,4},{4,5},{5,6},{6,7},{8,9},{9,10},{10,11},{11... | collective-permute-start | bytes 786440 | tf_op jit(solution)/shard_map/ppermute | solution.py:501
  8.7 1.8 fusion.2.refs_1_
  10.5 0.7 fusion.3.refs_2_
  11.2 0.1 copy.24
  11.4 0.7 maximum_bitcast_fusion.refs_0_
  12.1 0.6 fusion.7.refs_3_
  12.7 144.7 %gather_all.1 = (bf16[32,4,128,256]{3,2,1,0:T(8,128)(2,1)}, bf16[32,3,168,256]{3,2,1,0:T(8,128)(2,1)}, bf16[32,3,160,256]{3,2,1,0:T(8,128)(2,1)}, bf16[32,16,256]{2,1,0:T(8,128)(2,1)}) custom-call(bf16[1,4,128,256]{3,2,1,0:T(8,128)(2,1)} %maximum_bitcast_fusion.refs_0_, bf16[1,3,168,256]{3,2,1,0:T(8,128)(2,1)} %fusion.2.refs_1_, ...), custom_call_target="tpu_custom_call" | custom-call | tf_op jit(solution)/shard_map/gather_all/pallas_call | solution.py:138
  157.4 0.8 slice_bitcast_fusion.9
  158.2 0.1 reduce_sum.85
  158.3 0.2 multiply_reduce_fusion.2
  158.6 0.1 fusion.8
  158.7 0.3 multiply_sine_fusion
  158.9 0.6 fusion.11
  159.7 0.5 broadcast_in_dim.60.segk_ref
  160.3 0.8 copy.25.cos_ref
  161.1 0.8 copy.26.sin_ref
  161.9 0.8 copy.27.segq_ref
  162.7 0.1 pad.22.clone
  162.8 1.3 pad_maximum_fusion.x_ref
  164.1 24.0 %attend.1 = (f32[256,1024]{1,0:T(8,128)}, bf16[8,3,384,128]{3,2,1,0:T(8,128)(2,1)}, bf16[8,256,128]{2,1,0:T(8,128)(2,1)}, f32[8,256,2]{2,1,0:T(8,128)}) custom-call(f32[384,1024]{1,0:T(8,128)} %pad_maximum_fusion.x_ref, bf16[1,1024]{1,0:T(2,128)(2,1)} %bitcast.92, bf16[2,2,2,2,2,4,128,256]{7,6,5,4,3,2,1,0:T(8,128)(2,1)} %bitcast.99, ...), custom_call_target="tpu_custom_call" | custom-call | flops 3221225472 | bytes 8388608 | tf_op jit(solution)/shard_map/attend/pallas_call | solution.py:554
  188.1 1.4 reduce_sum.81
  189.6 0.1 copy-done.1
  189.7 0.2 multiply_reduce_fusion.4
  189.9 1.1 broadcast_in_dim.61.da0_ref
  191.0 20.8 %feed.2 = (bf16[2,2,2,2,2,3,168,256]{7,6,5,4,3,2,1,0:T(8,128)(2,1)}, f32[256,1024]{1,0:T(8,128)}, f32[256,1024]{1,0:T(8,128)}) custom-call(f32[256,1024]{1,0:T(8,128)} %get-tuple-element.31.y_ref.out0_ref, bf16[1,1024]{1,0:T(2,128)(2,1)} %bitcast.94, f32[256,1024]{1,0:T(8,128)} %bitcast.76, bf16[2,2,2,2,2,3,168,256]{7,6,5,4,3,2,1,0:T(8,128)(2,1)} %bitcast.101, ...), custom_call_target="tpu_custom_call" | custom-call | flops 6341787648 | bytes 16515072 | tf_op jit(solution)/shard_map/feed/pallas_call | solution.py:582
  211.8 20.5 %feed.3 = (bf16[2,2,2,2,2,3,160,256]{7,6,5,4,3,2,1,0:T(8,128)(2,1)}, f32[256,1024]{1,0:T(8,128)}, f32[256,1024]{1,0:T(8,128)}) custom-call(f32[256,1024]{1,0:T(8,128)} %get-tuple-element.31.y_ref.out0_ref, bf16[1,1024]{1,0:T(2,128)(2,1)} %bitcast.95, f32[256,1024]{1,0:T(8,128)} %bitcast.77, bf16[2,2,2,2,2,3,160,256]{7,6,5,4,3,2,1,0:T(8,128)(2,1)} %bitcast.102, ...), custom_call_target="tpu_custom_call" | custom-call | flops 6039797760 | bytes 15728640 | tf_op jit(solution)/shard_map/feed/pallas_call | solution.py:582
  232.4 1.8 multiply_reduce_fusion
  234.2 2.6 multiply_add_fusion.dy_ref
  236.7 30.4 %attend_back.1 = (bf16[2,2,2,2,2,4,128,256]{7,6,5,4,3,2,1,0:T(8,128)(2,1)}, f32[384,1024]{1,0:T(8,128)}, f32[1,1024]{1,0:T(1,128)}) custom-call(f32[384,1024]{1,0:T(8,128)} %pad_maximum_fusion.x_ref, bf16[1,1024]{1,0:T(2,128)(2,1)} %bitcast.93, bf16[2,2,2,2,2,4,128,256]{7,6,5,4,3,2,1,0:T(8,128)(2,1)} %bitcast.100, f32[384,128]{1,0:T(8,128)} %copy.25.cos_ref, ...), custom_call_target="tpu_custom_call" | custom-call | flops 6442450944 | bytes 16777216 | tf_op jit(solution)/shard_map/attend_back/pallas_call | solution.py:617
  267.2 0.5 broadcast.145
  267.7 1.3 reduce.4
  269.1 0.7 broadcast_in_dim.66
  269.9 140.7 %scatter_all.1 = (f32[4,128,256]{2,1,0:T(8,128)}, f32[3,168,256]{2,1,0:T(8,128)}, f32[3,160,256]{2,1,0:T(8,128)}, f32[8,256]{1,0:T(8,128)}) custom-call(bf16[32,4,128,256]{3,2,1,0:T(8,128)(2,1)} %bitcast.70, bf16[32,3,168,256]{3,2,1,0:T(8,128)(2,1)} %bitcast.71, bf16[32,3,160,256]{3,2,1,0:T(8,128)(2,1)} %bitcast.72, f32[32,8,256]{2,1,0:T(8,128)} %bitcast.75), custom_call_target="tpu_custom_call" | custom-call | tf_op jit(solution)/shard_map/scatter_all/pallas_call | solution.py:250
  410.6 1.1 slice_bitcast_fusion.1
  411.6 1.6 slice_bitcast_fusion.5
  413.2 1.1 constant_dynamic-update-slice_fusion.1
  414.4 0.9 slice_bitcast_fusion
  415.2 0.7 slice_bitcast_fusion.2
  416.0 0.1 convert.6
  416.1 1.3 collective-permute-start.3
  417.4 4.6 %collective-permute-start.2 = (bf16[64,1024]{1,0:T(8,128)(2,1)S(1)}, bf16[64,1024]{1,0:T(8,128)(2,1)S(1)}, u32[]{:S(2)}, u32[]{:S(2)}) collective-permute-start(bf16[64,1024]{1,0:T(8,128)(2,1)S(1)} %get-tuple-element.77), channel_id=1, source_target_pairs={{0,1},{1,2},{2,3},{3,4},{4,5},{5,6},{6,7},{8,9},{9,10},{10,11},{11... | collective-permute-start | bytes 393224 | tf_op jit(solution)/shard_map/ppermute | solution.py:663
  422.0 0.9 copy.32
  422.9 1.3 fusion.13
  424.3 1.3 collective-permute-done.2
  425.6 0.5 fusion.9
  426.1 1.4 add_bitcast_fusion
  (57 shorter events, 0.5 us)
Async XLA Ops:
  0.6 9.8 %copy-start.6 = (bf16[256,2,328]{0,2,1:T(8,128)(2,1)S(1)}, bf16[256,2,328]{0,2,1:T(8,128)(2,1)}, u32[]{:S(2)}) copy-start(bf16[256,2,328]{0,2,1:T(8,128)(2,1)} %param.17) | copy-start | bytes 1007620
  0.6 9.8 %copy-start.7 = (bf16[328,256]{1,0:T(8,128)(2,1)S(1)}, bf16[328,256]{1,0:T(8,128)(2,1)}, u32[]{:S(2)}) copy-start(bf16[328,256]{1,0:T(8,128)(2,1)} %param.18) | copy-start | bytes 503812
  0.7 10.5 %copy-start.9 = (bf16[256,3,128]{2,0,1:T(8,128)(2,1)S(1)}, bf16[256,3,128]{2,0,1:T(8,128)(2,1)}, u32[]{:S(2)}) copy-start(bf16[256,3,128]{2,0,1:T(8,128)(2,1)} %param.15) | copy-start | bytes 589828
  0.7 10.7 %copy-start.13 = (bf16[256]{0:T(256)(128)(2,1)S(1)}, bf16[256]{0:T(256)(128)(2,1)}, u32[]{:S(2)}) copy-start(bf16[256]{0:T(256)(128)(2,1)} %param.14) | copy-start | bytes 1540
  0.7 10.7 %copy-start.14 = (bf16[256]{0:T(256)(128)(2,1)S(1)}, bf16[256]{0:T(256)(128)(2,1)}, u32[]{:S(2)}) copy-start(bf16[256]{0:T(256)(128)(2,1)} %param.13) | copy-start | bytes 1540
  0.7 10.7 %copy-start.10 = (bf16[128,256]{1,0:T(8,128)(2,1)S(1)}, bf16[128,256]{1,0:T(8,128)(2,1)}, u32[]{:S(2)}) copy-start(bf16[128,256]{1,0:T(8,128)(2,1)} %param.16) | copy-start | bytes 196612
  1.8 161.0 %collective-permute-start.1 = (f32[64,1024]{1,0:T(8,128)S(1)}, f32[64,1024]{1,0:T(8,128)S(1)}, u32[]{:S(2)}, u32[]{:S(2)}) collective-permute-start(f32[64,1024]{1,0:T(8,128)S(1)} %get-tuple-element.76), channel_id=1, source_target_pairs={{1,0},{2,1},{3,2},{4,3},{5,4},{6,5},{7,6},{9,8},{10,9},{11,10},{12... | collective-permute-start | bytes 786440 | tf_op jit(solution)/shard_map/ppermute | solution.py:502
  3.1 159.7 %collective-permute-start = (f32[64,1024]{1,0:T(8,128)S(1)}, f32[64,1024]{1,0:T(8,128)S(1)}, u32[]{:S(2)}, u32[]{:S(2)}) collective-permute-start(f32[64,1024]{1,0:T(8,128)S(1)} %get-tuple-element.75), channel_id=1, source_target_pairs={{0,1},{1,2},{2,3},{3,4},{4,5},{5,6},{6,7},{8,9},{9,10},{10,11},{11... | collective-permute-start | bytes 786440 | tf_op jit(solution)/shard_map/ppermute | solution.py:501
  8.7 149.5 %copy-start = (f32[1,256,1024]{2,1,0:T(8,128)S(1)}, f32[1,256,1024]{2,1,0:T(8,128)}, u32[]{:S(2)}) copy-start(f32[1,256,1024]{2,1,0:T(8,128)} %param.10) | copy-start | bytes 3145732
  12.1 146.5 %copy-start.11 = (s32[1,2048]{1,0:T(1,128)S(1)}, s32[1,2048]{1,0:T(1,128)}, u32[]{:S(2)}) copy-start(s32[1,2048]{1,0:T(1,128)} %param.12) | copy-start | bytes 24580
  12.1 147.4 %copy-start.12 = (s32[1,2048]{1,0:T(1,128)S(1)}, s32[1,2048]{1,0:T(1,128)}, u32[]{:S(2)}) copy-start(s32[1,2048]{1,0:T(1,128)} %param.11) | copy-start | bytes 24580
  188.1 1.5 copy-start.1
  211.8 20.5 %copy-start.2 = (f32[256,1024]{1,0:T(8,128)S(1)}, f32[256,1024]{1,0:T(8,128)}, u32[]{:S(2)}) copy-start(f32[256,1024]{1,0:T(8,128)} %get-tuple-element.31.y_ref.out0_ref) | copy-start | bytes 3145732
  232.4 1.8 copy-start.4
  410.6 3.7 copy-start.8
  414.3 1.7 copy-start.3
  416.1 8.1 %collective-permute-start.3 = (bf16[64,1024]{1,0:T(8,128)(2,1)S(1)}, bf16[64,1024]{1,0:T(8,128)(2,1)S(1)}, u32[]{:S(2)}, u32[]{:S(2)}) collective-permute-start(bf16[64,1024]{1,0:T(8,128)(2,1)S(1)} %get-tuple-element.78), channel_id=1, source_target_pairs={{1,0},{2,1},{3,2},{4,3},{5,4},{6,5},{7,6},{9,8},{10,9},{11,10},{12... | collective-permute-start | bytes 393224 | tf_op jit(solution)/shard_map/ppermute | solution.py:662
  417.4 8.1 %collective-permute-start.2 = (bf16[64,1024]{1,0:T(8,128)(2,1)S(1)}, bf16[64,1024]{1,0:T(8,128)(2,1)S(1)}, u32[]{:S(2)}, u32[]{:S(2)}) collective-permute-start(bf16[64,1024]{1,0:T(8,128)(2,1)S(1)} %get-tuple-element.77), channel_id=1, source_target_pairs={{0,1},{1,2},{2,3},{3,4},{4,5},{5,6},{6,7},{8,9},{9,10},{10,11},{11... | collective-permute-start | bytes 393224 | tf_op jit(solution)/shard_map/ppermute | solution.py:663
  424.3 1.8 copy-start.5

commit v3 on v2

--- a/solution.py
+++ b/solution.py
@@ -108,27 +108,36 @@
     ]
     for load in loads:
         load.start()
+    lanes = []
+    for i in range(count):
+        parts = outs[i].shape[1]
+        cut = (parts + i % 2) // 2 if len(outs[i].shape) == 4 else parts
+        lanes.append((0, i, pl.ds(0, cut)))
+        if cut < parts:
+            lanes.append((1, i, pl.ds(cut, parts - cut)))
+    lanes.sort(key=lambda lane: lane[:2])
+    flying = {}
     for s in range(bits - 1, -1, -1):
         size = 2 ** (bits - 1 - s)
-        copies = []
-        for i, order in enumerate(orders):
-            base = (spots[i] // size) * size
-            span = outs[i].at[pl.ds(base, size)]
+        for group, i, rows in lanes:
+            if (group, i) in flying:
+                flying[group, i].wait()
+            span = outs[i].at[pl.ds((spots[i] // size) * size, size), rows]
             copy = pltpu.make_async_remote_copy(
-                src_ref=ins[i] if size == 1 else span,
+                src_ref=ins[i].at[pl.ds(0, 1), rows] if size == 1 else span,
                 dst_ref=span,
-                send_sem=send_sem.at[i, s],
-                recv_sem=recv_sem.at[i, s],
-                device_id=partner(*order[s]),
+                send_sem=send_sem.at[group, i, s],
+                recv_sem=recv_sem.at[group, i, s],
+                device_id=partner(*orders[i][s]),
                 device_id_type=pl.DeviceIdType.MESH,
             )
             copy.start()
-            copies.append(copy)
+            flying[group, i] = copy
         if s == bits - 1:
             for load in loads:
                 load.wait()
-        for copy in copies:
-            copy.wait()
+    for copy in flying.values():
+        copy.wait()
 
 
 def gather_all(orders, dps, tensors, shards):
@@ -142,10 +151,11 @@
         out_shape=[jax.ShapeDtypeStruct((group,) + x.shape, x.dtype) for x in shards],
         scratch_shapes=[
             pltpu.SemaphoreType.DMA((count,)),
-            pltpu.SemaphoreType.DMA((count, bits)),
-            pltpu.SemaphoreType.DMA((count, bits)),
+            pltpu.SemaphoreType.DMA((2, count, bits)),
+            pltpu.SemaphoreType.DMA((2, count, bits)),
         ],
         compiler_params=pltpu.CompilerParams(collective_id=0, has_side_effects=True),
+        cost_estimate=cost(0, 3 * 10**8),
         name="gather_all",
     )(*[x[None] for x in shards])
 
@@ -200,11 +210,10 @@
         return copy
 
     loads = [[load(i, c) for c in range(2)] for i in range(count)]
-    for copy in copies:
-        copy.wait()
     later = []
-    for c in range(pieces):
-        for i in range(count):
+    for i in range(count):
+        copies[i].wait()
+        for c in range(pieces):
             loads[i][c].wait()
             at = start_of(i, c)
 
@@ -262,6 +271,7 @@
         compiler_params=pltpu.CompilerParams(
             collective_id=1, has_side_effects=True, vmem_limit_bytes=60 * 1024 * 1024
         ),
+        cost_estimate=cost(0, 3 * 10**8),
         name="scatter_all",
     )(*parts)
 

time: 429 us -> 405 us (0.944)
  Pallas kernels: 381 us -> 358 us
    pallas_call x1, Pallas kernels: 145 us -> 126 us  [gather_all(): pl.pallas_call(functools.partial(gather_kernel, orders), in_specs=[pl.Blo...]
    pallas_call x1, Pallas kernels: 141 us -> 136 us  [scatter_all(): pl.pallas_call(functools.partial(scatter_kernel, orders), in_specs=[pl.Bl...]
  transfers between devices with their start and end apart: 4 -> 4, of which waited for: 1 -> 1; matrix products, arithmetic and copies ran while one was open for 3% -> 3% of each run, Pallas kernels for 34% -> 31%
where the time goes in v3:
time: 405 us; the launch traced here: 403 us
  Pallas kernels  358 us (88%)
  other arithmetic  15.9 us (4%)
  local copies, waits for them, and re-layouts  15.7 us (4%)
  starting transfers between devices  12.7 us (3%)
    pallas_call x1, Pallas kernels, scatter_all(): pl.pallas_call(functools.partial(scatter_kernel, orders), in_specs=[pl.Bl...  136 us
    pallas_call x1, Pallas kernels, gather_all(): pl.pallas_call(functools.partial(gather_kernel, orders), in_specs=[pl.Blo...  126 us
    pallas_call x2, Pallas kernels, body(): pl.pallas_call(functools.partial(feed_kernel, order, dps), grid=(tensors,...  41.3 us
    pallas_call x1, Pallas kernels, body(): pl.pallas_call(functools.partial(attend_back_kernel, orders[0], dps), gri...  30.4 us
    pallas_call x1, Pallas kernels, body(): pl.pallas_call(functools.partial(attend_kernel, orders[0], dps), grid=(te...  24 us
  transfers between devices with their start and end apart: 4, of which 1 were waited for; matrix products, arithmetic and copies ran while one was open for 3% of the time, Pallas kernels for 31%

profile of v3, /device:TPU:0, one launch (start us, length us, event | category | flops | bytes accessed | tf_op | source)
XLA Modules:
  0.0 403.5 jit_solution(3254002997429962593)
XLA Ops:
  0.7 1.1 slice_bitcast_fusion.4
  1.8 1.3 collective-permute-start.1
  3.1 5.5 %collective-permute-start = (f32[64,1024]{1,0:T(8,128)S(1)}, f32[64,1024]{1,0:T(8,128)S(1)}, u32[]{:S(2)}, u32[]{:S(2)}) collective-permute-start(f32[64,1024]{1,0:T(8,128)S(1)} %get-tuple-element.75), channel_id=1, source_target_pairs={{0,1},{1,2},{2,3},{3,4},{4,5},{5,6},{6,7},{8,9},{9,10},{10,11},{11... | collective-permute-start | bytes 786440 | tf_op jit(solution)/shard_map/ppermute | solution.py:511
  8.7 1.8 fusion.2.refs_1_
  10.5 0.7 fusion.3.refs_2_
  11.2 0.1 copy.24
  11.4 0.7 maximum_bitcast_fusion.refs_0_
  12.1 0.6 fusion.7.refs_3_
  12.7 126.1 %gather_all.1 = (bf16[32,4,128,256]{3,2,1,0:T(8,128)(2,1)}, bf16[32,3,168,256]{3,2,1,0:T(8,128)(2,1)}, bf16[32,3,160,256]{3,2,1,0:T(8,128)(2,1)}, bf16[32,16,256]{2,1,0:T(8,128)(2,1)}) custom-call(bf16[1,4,128,256]{3,2,1,0:T(8,128)(2,1)} %maximum_bitcast_fusion.refs_0_, bf16[1,3,168,256]{3,2,1,0:T(8,128)(2,1)} %fusion.2.refs_1_, ...), custom_call_target="tpu_custom_call" | custom-call | bytes 300000000 | tf_op jit(solution)/shard_map/gather_all/pallas_call | solution.py:147
  138.9 0.8 slice_bitcast_fusion.9
  139.6 0.1 reduce_sum.85
  139.8 0.2 multiply_reduce_fusion.2
  140.0 0.1 fusion.8
  140.1 0.3 multiply_sine_fusion
  140.4 0.6 fusion.11
  141.1 0.5 broadcast_in_dim.60.segk_ref
  141.7 0.8 copy.25.cos_ref
  142.5 0.8 copy.26.sin_ref
  143.3 0.8 copy.27.segq_ref
  144.1 0.1 pad.22.clone
  144.2 1.3 pad_maximum_fusion.x_ref
  145.6 24.0 %attend.1 = (f32[256,1024]{1,0:T(8,128)}, bf16[8,3,384,128]{3,2,1,0:T(8,128)(2,1)}, bf16[8,256,128]{2,1,0:T(8,128)(2,1)}, f32[8,256,2]{2,1,0:T(8,128)}) custom-call(f32[384,1024]{1,0:T(8,128)} %pad_maximum_fusion.x_ref, bf16[1,1024]{1,0:T(2,128)(2,1)} %bitcast.92, bf16[2,2,2,2,2,4,128,256]{7,6,5,4,3,2,1,0:T(8,128)(2,1)} %bitcast.99, ...), custom_call_target="tpu_custom_call" | custom-call | flops 3221225472 | bytes 8388608 | tf_op jit(solution)/shard_map/attend/pallas_call | solution.py:564
  169.6 1.4 reduce_sum.81
  171.1 0.2 multiply_reduce_fusion.4
  171.4 1.1 broadcast_in_dim.61.da0_ref
  172.5 20.8 %feed.2 = (bf16[2,2,2,2,2,3,168,256]{7,6,5,4,3,2,1,0:T(8,128)(2,1)}, f32[256,1024]{1,0:T(8,128)}, f32[256,1024]{1,0:T(8,128)}) custom-call(f32[256,1024]{1,0:T(8,128)} %get-tuple-element.31.y_ref.out0_ref, bf16[1,1024]{1,0:T(2,128)(2,1)} %bitcast.94, f32[256,1024]{1,0:T(8,128)} %bitcast.76, bf16[2,2,2,2,2,3,168,256]{7,6,5,4,3,2,1,0:T(8,128)(2,1)} %bitcast.101, ...), custom_call_target="tpu_custom_call" | custom-call | flops 6341787648 | bytes 16515072 | tf_op jit(solution)/shard_map/feed/pallas_call | solution.py:592
  193.3 20.5 %feed.3 = (bf16[2,2,2,2,2,3,160,256]{7,6,5,4,3,2,1,0:T(8,128)(2,1)}, f32[256,1024]{1,0:T(8,128)}, f32[256,1024]{1,0:T(8,128)}) custom-call(f32[256,1024]{1,0:T(8,128)} %get-tuple-element.31.y_ref.out0_ref, bf16[1,1024]{1,0:T(2,128)(2,1)} %bitcast.95, f32[256,1024]{1,0:T(8,128)} %bitcast.77, bf16[2,2,2,2,2,3,160,256]{7,6,5,4,3,2,1,0:T(8,128)(2,1)} %bitcast.102, ...), custom_call_target="tpu_custom_call" | custom-call | flops 6039797760 | bytes 15728640 | tf_op jit(solution)/shard_map/feed/pallas_call | solution.py:592
  213.8 1.8 multiply_reduce_fusion
  215.6 2.6 multiply_add_fusion.dy_ref
  218.2 30.4 %attend_back.1 = (bf16[2,2,2,2,2,4,128,256]{7,6,5,4,3,2,1,0:T(8,128)(2,1)}, f32[384,1024]{1,0:T(8,128)}, f32[1,1024]{1,0:T(1,128)}) custom-call(f32[384,1024]{1,0:T(8,128)} %pad_maximum_fusion.x_ref, bf16[1,1024]{1,0:T(2,128)(2,1)} %bitcast.93, bf16[2,2,2,2,2,4,128,256]{7,6,5,4,3,2,1,0:T(8,128)(2,1)} %bitcast.100, f32[384,128]{1,0:T(8,128)} %copy.25.cos_ref, ...), custom_call_target="tpu_custom_call" | custom-call | flops 6442450944 | bytes 16777216 | tf_op jit(solution)/shard_map/attend_back/pallas_call | solution.py:627
  248.6 0.5 broadcast.145
  249.1 1.3 reduce.4
  250.6 0.7 broadcast_in_dim.66
  251.3 135.8 %scatter_all.1 = (f32[4,128,256]{2,1,0:T(8,128)}, f32[3,168,256]{2,1,0:T(8,128)}, f32[3,160,256]{2,1,0:T(8,128)}, f32[8,256]{1,0:T(8,128)}) custom-call(bf16[32,4,128,256]{3,2,1,0:T(8,128)(2,1)} %bitcast.70, bf16[32,3,168,256]{3,2,1,0:T(8,128)(2,1)} %bitcast.71, bf16[32,3,160,256]{3,2,1,0:T(8,128)(2,1)} %bitcast.72, f32[32,8,256]{2,1,0:T(8,128)} %bitcast.75), custom_call_target="tpu_custom_call" | custom-call | bytes 300000000 | tf_op jit(solution)/shard_map/scatter_all/pallas_call | solution.py:259
  387.1 1.1 slice_bitcast_fusion.1
  388.2 1.6 slice_bitcast_fusion.5
  389.8 1.1 constant_dynamic-update-slice_fusion.1
  390.9 0.9 slice_bitcast_fusion
  391.8 0.7 slice_bitcast_fusion.2
  392.6 0.1 convert.6
  392.7 1.3 collective-permute-start.3
  394.0 4.6 %collective-permute-start.2 = (bf16[64,1024]{1,0:T(8,128)(2,1)S(1)}, bf16[64,1024]{1,0:T(8,128)(2,1)S(1)}, u32[]{:S(2)}, u32[]{:S(2)}) collective-permute-start(bf16[64,1024]{1,0:T(8,128)(2,1)S(1)} %get-tuple-element.77), channel_id=1, source_target_pairs={{0,1},{1,2},{2,3},{3,4},{4,5},{5,6},{6,7},{8,9},{9,10},{10,11},{11... | collective-permute-start | bytes 393224 | tf_op jit(solution)/shard_map/ppermute | solution.py:673
  398.6 0.9 copy.32
  399.5 1.3 fusion.13
  400.9 0.5 collective-permute-done.2
  401.4 0.5 fusion.9
  401.9 0.2 copy-done.5
  402.1 1.4 add_bitcast_fusion
  (57 shorter events, 0.5 us)
Async XLA Ops:
  0.6 9.8 %copy-start.6 = (bf16[256,2,328]{0,2,1:T(8,128)(2,1)S(1)}, bf16[256,2,328]{0,2,1:T(8,128)(2,1)}, u32[]{:S(2)}) copy-start(bf16[256,2,328]{0,2,1:T(8,128)(2,1)} %param.17) | copy-start | bytes 1007620
  0.6 9.8 %copy-start.7 = (bf16[328,256]{1,0:T(8,128)(2,1)S(1)}, bf16[328,256]{1,0:T(8,128)(2,1)}, u32[]{:S(2)}) copy-start(bf16[328,256]{1,0:T(8,128)(2,1)} %param.18) | copy-start | bytes 503812
  0.7 10.5 %copy-start.9 = (bf16[256,3,128]{2,0,1:T(8,128)(2,1)S(1)}, bf16[256,3,128]{2,0,1:T(8,128)(2,1)}, u32[]{:S(2)}) copy-start(bf16[256,3,128]{2,0,1:T(8,128)(2,1)} %param.15) | copy-start | bytes 589828
  0.7 10.7 %copy-start.13 = (bf16[256]{0:T(256)(128)(2,1)S(1)}, bf16[256]{0:T(256)(128)(2,1)}, u32[]{:S(2)}) copy-start(bf16[256]{0:T(256)(128)(2,1)} %param.14) | copy-start | bytes 1540
  0.7 10.7 %copy-start.14 = (bf16[256]{0:T(256)(128)(2,1)S(1)}, bf16[256]{0:T(256)(128)(2,1)}, u32[]{:S(2)}) copy-start(bf16[256]{0:T(256)(128)(2,1)} %param.13) | copy-start | bytes 1540
  0.7 10.7 %copy-start.10 = (bf16[128,256]{1,0:T(8,128)(2,1)S(1)}, bf16[128,256]{1,0:T(8,128)(2,1)}, u32[]{:S(2)}) copy-start(bf16[128,256]{1,0:T(8,128)(2,1)} %param.16) | copy-start | bytes 196612
  1.8 142.4 %collective-permute-start.1 = (f32[64,1024]{1,0:T(8,128)S(1)}, f32[64,1024]{1,0:T(8,128)S(1)}, u32[]{:S(2)}, u32[]{:S(2)}) collective-permute-start(f32[64,1024]{1,0:T(8,128)S(1)} %get-tuple-element.76), channel_id=1, source_target_pairs={{1,0},{2,1},{3,2},{4,3},{5,4},{6,5},{7,6},{9,8},{10,9},{11,10},{12... | collective-permute-start | bytes 786440 | tf_op jit(solution)/shard_map/ppermute | solution.py:512
  3.1 141.1 %collective-permute-start = (f32[64,1024]{1,0:T(8,128)S(1)}, f32[64,1024]{1,0:T(8,128)S(1)}, u32[]{:S(2)}, u32[]{:S(2)}) collective-permute-start(f32[64,1024]{1,0:T(8,128)S(1)} %get-tuple-element.75), channel_id=1, source_target_pairs={{0,1},{1,2},{2,3},{3,4},{4,5},{5,6},{6,7},{8,9},{9,10},{10,11},{11... | collective-permute-start | bytes 786440 | tf_op jit(solution)/shard_map/ppermute | solution.py:511
  8.7 131.0 %copy-start = (f32[1,256,1024]{2,1,0:T(8,128)S(1)}, f32[1,256,1024]{2,1,0:T(8,128)}, u32[]{:S(2)}) copy-start(f32[1,256,1024]{2,1,0:T(8,128)} %param.10) | copy-start | bytes 3145732
  12.1 127.9 %copy-start.11 = (s32[1,2048]{1,0:T(1,128)S(1)}, s32[1,2048]{1,0:T(1,128)}, u32[]{:S(2)}) copy-start(s32[1,2048]{1,0:T(1,128)} %param.12) | copy-start | bytes 24580
  12.1 128.9 %copy-start.12 = (s32[1,2048]{1,0:T(1,128)S(1)}, s32[1,2048]{1,0:T(1,128)}, u32[]{:S(2)}) copy-start(s32[1,2048]{1,0:T(1,128)} %param.11) | copy-start | bytes 24580
  169.6 1.5 copy-start.1
  193.3 20.5 %copy-start.2 = (f32[256,1024]{1,0:T(8,128)S(1)}, f32[256,1024]{1,0:T(8,128)}, u32[]{:S(2)}) copy-start(f32[256,1024]{1,0:T(8,128)} %get-tuple-element.31.y_ref.out0_ref) | copy-start | bytes 3145732
  213.8 1.8 copy-start.4
  387.1 3.7 copy-start.8
  390.9 1.7 copy-start.3
  392.7 8.1 %collective-permute-start.3 = (bf16[64,1024]{1,0:T(8,128)(2,1)S(1)}, bf16[64,1024]{1,0:T(8,128)(2,1)S(1)}, u32[]{:S(2)}, u32[]{:S(2)}) collective-permute-start(bf16[64,1024]{1,0:T(8,128)(2,1)S(1)} %get-tuple-element.78), channel_id=1, source_target_pairs={{1,0},{2,1},{3,2},{4,3},{5,4},{6,5},{7,6},{9,8},{10,9},{11,10},{12... | collective-permute-start | bytes 393224 | tf_op jit(solution)/shard_map/ppermute | solution.py:672
  394.0 7.3 %collective-permute-start.2 = (bf16[64,1024]{1,0:T(8,128)(2,1)S(1)}, bf16[64,1024]{1,0:T(8,128)(2,1)S(1)}, u32[]{:S(2)}, u32[]{:S(2)}) collective-permute-start(bf16[64,1024]{1,0:T(8,128)(2,1)S(1)} %get-tuple-element.77), channel_id=1, source_target_pairs={{0,1},{1,2},{2,3},{3,4},{4,5},{5,6},{6,7},{8,9},{9,10},{10,11},{11... | collective-permute-start | bytes 393224 | tf_op jit(solution)/shard_map/ppermute | solution.py:673
  400.9 1.2 copy-start.5
